TPU v7x, 256 devices: a whole 4x4x8 slice. The times are simulated.
256 devices in a mesh: gx: 16 (over x, y_lo, core), gy: 16 (over y_hi, z).
Axes of the slice: x: 4, y: 4 (y_hi: 2, y_lo: 2; y = y_hi * 2 + y_lo), z: 8, core: 2. Of those that a mesh axis runs over, the one named last changes fastest.
Arguments:
- wave_fields: float32 [9, 32, 128, 2048], P(None, None, 'gy', 'gx'), may hold values from -6 to 6
- lame_lambda: float32 [32, 128, 2048], P(None, 'gy', 'gx'), may hold values from 0.5 to 1
- shear_modulus: float32 [32, 128, 2048], P(None, 'gy', 'gx'), may hold values from 0.3 to 0.7
- buoyancy: float32 [32, 128, 2048], P(None, 'gy', 'gx'), may hold values from 0.5 to 1
- ocean_state: float32 [3, 128, 2048], P(None, 'gy', 'gx'), may hold values from -6 to 6
- water_depth: float32 [128, 2048], P('gy', 'gx'), may hold values from 0.5 to 2
- seafloor_index: int32 [128, 2048], P('gy', 'gx'), may hold values from 0 to 15
- wet_mask: int32 [128, 2048], P('gy', 'gx'), may hold values 0 or 1
Outputs:
- wave_out: float32 [9, 32, 128, 2048], P(None, None, 'gy', 'gx')
- ocean_out: float32 [3, 128, 2048], P(None, 'gy', 'gx')
All inputs are finite; a program needn't handle non-finite values. No bound on the sum of `wet_mask` on one device may be relied on, other than what follows from the above.
Results may differ from a plain program's by a relative error of at most 0.0001.
Values sent between devices are 32-bit elements; how exact they have to be, the bound alone decides.
A program may use at most 64 MiB of HBM per device.

v0:
```python
import jax
import jax.numpy as jnp
from jax import lax
from jax.sharding import PartitionSpec as P

STEPS = 2


coef_near = 9.0 / 8.0
coef_far = -1.0 / 24.0
courant = 0.3
ocean_rate = 0.3
uplift = 0.5
loading = 0.5
viscous = 0.1


def extended(block, sides, width):
    for axis, dim in sides:
        count = lax.axis_size(axis)
        forward = [(i, i + 1) for i in range(count - 1)]
        backward = [(target, source) for source, target in forward]
        low = lax.ppermute(
            lax.slice_in_dim(block, block.shape[dim] - width, None, axis=dim), axis, forward
        )
        high = lax.ppermute(lax.slice_in_dim(block, 0, width, axis=dim), axis, backward)
        block = jnp.concatenate([low, block, high], axis=dim)
    return block


def differ(padded, direction, margins, forward):
    extent = padded.shape

    def sample(offset):
        selector = []
        for dimension in range(3):
            margin = margins[dimension]
            if dimension == direction:
                selector.append(slice(margin + offset, extent[dimension] - margin + offset))
            else:
                selector.append(slice(margin, extent[dimension] - margin))
        return padded[tuple(selector)]

    if forward:
        return coef_near * (sample(1) - sample(0)) + coef_far * (sample(2) - sample(-1))
    return coef_near * (sample(0) - sample(-1)) + coef_far * (sample(1) - sample(-2))


def advance_velocity(velocity, stress_pad, buoyancy, margins):
    stress_xx, stress_yy, stress_zz = (stress_pad[0], stress_pad[1], stress_pad[2])
    stress_xy, stress_xz, stress_yz = (stress_pad[3], stress_pad[4], stress_pad[5])
    accel_x = (
        differ(stress_xx, 2, margins, True)
        + differ(stress_xy, 1, margins, False)
        + differ(stress_xz, 0, margins, False)
    )
    accel_y = (
        differ(stress_xy, 2, margins, False)
        + differ(stress_yy, 1, margins, True)
        + differ(stress_yz, 0, margins, False)
    )
    accel_z = (
        differ(stress_xz, 2, margins, False)
        + differ(stress_yz, 1, margins, False)
        + differ(stress_zz, 0, margins, True)
    )
    return jnp.stack(
        [
            velocity[0] + courant * buoyancy * accel_x,
            velocity[1] + courant * buoyancy * accel_y,
            velocity[2] + courant * buoyancy * accel_z,
        ]
    )


def advance_stress(stress, velocity_pad, lame, shear, margins):
    speed_x, speed_y, speed_z = (velocity_pad[0], velocity_pad[1], velocity_pad[2])
    strain_x = differ(speed_x, 2, margins, False)
    strain_y = differ(speed_y, 1, margins, False)
    strain_z = differ(speed_z, 0, margins, False)
    trace = strain_x + strain_y + strain_z
    shear_xy = differ(speed_x, 1, margins, True) + differ(speed_y, 2, margins, True)
    shear_xz = differ(speed_x, 0, margins, True) + differ(speed_z, 2, margins, True)
    shear_yz = differ(speed_y, 0, margins, True) + differ(speed_z, 1, margins, True)
    return jnp.stack(
        [
            stress[0] + courant * (lame * trace + 2.0 * shear * strain_x),
            stress[1] + courant * (lame * trace + 2.0 * shear * strain_y),
            stress[2] + courant * (lame * trace + 2.0 * shear * strain_z),
            stress[3] + courant * shear * shear_xy,
            stress[4] + courant * shear * shear_xz,
            stress[5] + courant * shear * shear_yz,
        ]
    )


def ocean_level(level, flux_pad, vertical, onehot, wet):
    seafloor = jnp.sum(vertical * onehot, axis=0)
    east = flux_pad[0]
    north = flux_pad[1]
    spread = 0.5 * (east[1:-1, 2:] - east[1:-1, :-2]) + 0.5 * (north[2:, 1:-1] - north[:-2, 1:-1])
    return level + wet * (uplift * seafloor - ocean_rate * spread)


def ocean_flux(fluxes, flux_pad, level_pad, depth, wet):
    slope_x = 0.5 * (level_pad[1:-1, 2:] - level_pad[1:-1, :-2])
    slope_y = 0.5 * (level_pad[2:, 1:-1] - level_pad[:-2, 1:-1])
    laplace = (
        flux_pad[:, 1:-1, 2:]
        + flux_pad[:, 1:-1, :-2]
        + flux_pad[:, 2:, 1:-1]
        + flux_pad[:, :-2, 1:-1]
        - 4.0 * fluxes
    )
    east = wet * (fluxes[0] - ocean_rate * depth * slope_x + viscous * laplace[0])
    north = wet * (fluxes[1] - ocean_rate * depth * slope_y + viscous * laplace[1])
    return jnp.stack([east, north])


def local(
    wave_fields,
    lame_lambda,
    shear_modulus,
    buoyancy,
    ocean_state,
    water_depth,
    seafloor_index,
    wet_mask,
):
    wet = wet_mask.astype(jnp.float32)
    layers = jnp.arange(wave_fields.shape[1], dtype=jnp.int32)
    onehot = (layers[:, None, None] == seafloor_index[None, :, :]).astype(jnp.float32)
    depth_pad = ((0, 0), (2, 2), (0, 0), (0, 0))
    fields = wave_fields
    ocean = ocean_state
    for number in range(STEPS):
        flux_pad = extended(ocean[1:3], (("gx", 2), ("gy", 1)), 1)
        stress = fields[3:9]
        stress_pad = extended(stress, (("gx", 3), ("gy", 2)), 2)
        stress_pad = jnp.pad(stress_pad, depth_pad)
        velocity = advance_velocity(fields[0:3], stress_pad, buoyancy, (2, 2, 2))
        velocity_pad = extended(velocity, (("gx", 3), ("gy", 2)), 2)
        velocity_pad = jnp.pad(velocity_pad, depth_pad)
        stress = advance_stress(stress, velocity_pad, lame_lambda, shear_modulus, (2, 2, 2))
        level = ocean_level(ocean[0], flux_pad, velocity[2], onehot, wet)
        level_pad = extended(level, (("gx", 1), ("gy", 0)), 1)
        fluxes = ocean_flux(ocean[1:3], flux_pad, level_pad, water_depth, wet)
        pressed = stress[2] - loading * onehot * (wet * level)[None, :, :]
        stress = jnp.concatenate([stress[0:2], pressed[None], stress[3:6]], axis=0)
        fields = jnp.concatenate([velocity, stress], axis=0)
        ocean = jnp.concatenate([level[None], fluxes], axis=0)
    return (fields, ocean)


def solution(mesh):
    in_specs = (
        P(None, None, "gy", "gx"),
        P(None, "gy", "gx"),
        P(None, "gy", "gx"),
        P(None, "gy", "gx"),
        P(None, "gy", "gx"),
        P("gy", "gx"),
        P("gy", "gx"),
        P("gy", "gx"),
    )
    out_specs = (P(None, None, "gy", "gx"), P(None, "gy", "gx"))
    return jax.shard_map(local, mesh=mesh, in_specs=in_specs, out_specs=out_specs, check_vma=False)
```

profile of v0, /device:TPU:18, one launch (start us, length us, event | category | flops | bytes accessed | tf_op | source)
XLA Modules:
  0.0 317.3 jit_solution(14435436908763883864)
XLA Ops:
  3.3 2.6 collective-permute-start.1
  6.9 1.9 collective-permute-start
  8.9 4.5 %collective-permute-start.9 = (f32[2,8,1]{2,1,0:T(8,128)S(1)}, f32[2,8,1]{2,1,0:T(8,128)S(1)}, u32[]{:S(2)}, u32[]{:S(2)}) collective-permute-start(f32[2,8,1]{2,1,0:T(8,128)S(1)} %get-tuple-element.97), channel_id=1, source_target_pairs={{16,0},{32,16},{48,32},{64,48},{80,64},{96,80},{112,96},{128,112},... | collective-permute-start | bytes 200 | tf_op jit(solution)/shard_map/ppermute | solution.py:26
  13.4 1.9 collective-permute-start.8
  19.4 7.8 %collective-permute-start.11 = (f32[2,1,130]{2,1,0:T(1,128)S(1)}, f32[2,1,130]{2,1,0:T(1,128)S(1)}, u32[]{:S(2)}, u32[]{:S(2)}) collective-permute-start(f32[2,1,130]{2,1,0:T(1,128)S(1)} %get-tuple-element.91), channel_id=1, source_target_pairs={{1,0},{2,1},{3,2},{4,3},{5,4},{6,5},{7,6},{8,7},{9,8},{10,9},{11,1... | collective-permute-start | bytes 3128 | tf_op jit(solution)/shard_map/ppermute | solution.py:26
  27.2 1.9 collective-permute-start.10
  40.3 2.0 copy.427
  43.8 7.5 %collective-permute-start.3 = (f32[6,32,2,132]{3,1,2,0:T(8,128)S(1)}, f32[6,32,2,132]{3,1,2,0:T(8,128)S(1)}, u32[]{:S(2)}, u32[]{:S(2)}) collective-permute-start(f32[6,32,2,132]{3,1,2,0:T(8,128)S(1)} %get-tuple-element.54), channel_id=1, source_target_pairs={{1,0},{2,1},{3,2},{4,3},{5,4},{6,5},{7,6},{8,7},{9,8},{10,9},{11,1... | collective-permute-start | bytes 608264 | tf_op jit(solution)/shard_map/ppermute | solution.py:26
  51.3 2.4 collective-permute-start.2
  54.5 3.6 %collective-permute-done.3 = f32[6,32,2,132]{3,1,2,0:T(8,128)S(1)} collective-permute-done((f32[6,32,2,132]{3,1,2,0:T(8,128)S(1)}, f32[6,32,2,132]{3,1,2,0:T(8,128)S(1)}, u32[]{:S(2)}, u32[]{:S(2)}) %collective-permute-start.3) | collective-permute-done | bytes 202784 | tf_op jit(solution)/shard_map/ppermute | solution.py:26
  58.0 7.7 %collective-permute-done.2 = f32[6,32,2,132]{3,1,2,0:T(8,128)S(1)} collective-permute-done((f32[6,32,2,132]{3,1,2,0:T(8,128)S(1)}, f32[6,32,2,132]{3,1,2,0:T(8,128)S(1)}, u32[]{:S(2)}, u32[]{:S(2)}) %collective-permute-start.2) | collective-permute-done | bytes 202784 | tf_op jit(solution)/shard_map/ppermute | solution.py:23
  65.8 2.2 pad_maximum_fusion
  68.0 6.7 %copy.429 = f32[6,32,12,132]{1,2,3,0:T(8,128)} copy(f32[6,32,12,132]{3,1,2,0:T(8,128)} %pad_maximum_fusion) | data formatting | bytes 2433024 | tf_op jit(solution)/shard_map/concatenate | solution.py:27
  74.7 6.1 %fusion.5 = (f32[36,12,132]{0,1,2:T(8,128)}, f32[36,12,132]{0,1,2:T(8,128)S(1)}, f32[36,12,132]{0,1,2:T(8,128)S(1)}, f32[36,12,132]{0,1,2:T(8,128)S(1)}, f32[36,12,132]{0,1,2:T(8,128)S(1)}, /*index=5*/f32[36,12,132]{0,1,2:T(8,128)}) fusion(f32[6,32,12,132]{1,2,3,0:T(8,128)} %copy.429), kind=kLoop, calls=%fused_computation.24 | loop fusion | bytes 2585088 | tf_op jit(solution)/shard_map/squeeze | solution.py:50
  80.8 3.3 %select_reduce_fusion.1 = (f32[8,128]{0,1:T(8,128)}, f32[32,8,128]{0,1,2:T(8,128)}) fusion(s32[8,128]{0,1:T(8,128)S(1)} %copy.443, f32[36,12,132]{0,1,2:T(8,128)S(1)} %get-tuple-element.41, f32[36,12,132]{0,1,2:T(8,128)S(1)} %get-tuple-element.40, f32[36,12,132]{0,1,2:T(8,128)S(1)} %get-tuple-element.39, f32[32,8,128]{0,1,2:T(8,128)S(1)} %copy.423, ...), kind=kLoop, calls=%fused_computation.289 | loop fusion | flops 752640 | bytes 1974272 | tf_op jit(solution)/shard_map/reduce_sum | solution.py:98
  85.3 6.7 %fusion.144 = f32[32,8,128]{0,1,2:T(8,128)} fusion(f32[36,12,132]{0,1,2:T(8,128)} %copy-done.1, f32[36,12,132]{0,1,2:T(8,128)} %get-tuple-element.37, f32[36,12,132]{0,1,2:T(8,128)S(1)} %get-tuple-element.38, f32[1,32,8,128]{1,2,3,0:T(8,128)} %copy.477, f32[32,8,128]{0,1,2:T(8,128)S(1)} %copy.423), kind=kLoop, calls=%fused_computation.243 | loop fusion | flops 655360 | bytes 1966080 | tf_op jit(solution)/shard_map/add | solution.py:70
  93.2 5.4 %fusion.157 = f32[32,8,128]{0,1,2:T(8,128)} fusion(f32[36,12,132]{0,1,2:T(8,128)S(1)} %get-tuple-element.39, f32[36,12,132]{0,1,2:T(8,128)S(1)} %get-tuple-element.38, f32[36,12,132]{0,1,2:T(8,128)} %get-tuple-element.42, f32[1,32,8,128]{1,2,3,0:T(8,128)} %copy.472, f32[32,8,128]{0,1,2:T(8,128)S(1)} %copy.423), kind=kLoop, calls=%fused_computation.262 | loop fusion | flops 655360 | bytes 1966080 | tf_op jit(solution)/shard_map/add | solution.py:69
  101.7 4.3 %collective-permute-start.20 = (f32[8,1]{1,0:T(8,128)S(1)}, f32[8,1]{1,0:T(8,128)S(1)}, u32[]{:S(2)}, u32[]{:S(2)}) collective-permute-start(f32[8,1]{1,0:T(8,128)S(1)} %get-tuple-element.102), channel_id=1, source_target_pairs={{16,0},{32,16},{48,32},{64,48},{80,64},{96,80},{112,96},{128,112},... | collective-permute-start | bytes 104 | tf_op jit(solution)/shard_map/ppermute | solution.py:26
  106.1 2.1 collective-permute-start.21
  108.2 3.9 %collective-permute-done.21 = f32[8,1]{1,0:T(8,128)S(1)} collective-permute-done((f32[8,1]{1,0:T(8,128)S(1)}, f32[8,1]{1,0:T(8,128)S(1)}, u32[]{:S(2)}, u32[]{:S(2)}) %collective-permute-start.21) | collective-permute-done | bytes 64 | tf_op jit(solution)/shard_map/ppermute | solution.py:23
  112.1 1.9 collective-permute-start.23
  114.1 7.5 %collective-permute-start.22 = (f32[1,130]{1,0:T(1,128)S(1)}, f32[1,130]{1,0:T(1,128)S(1)}, u32[]{:S(2)}, u32[]{:S(2)}) collective-permute-start(f32[1,130]{1,0:T(1,128)S(1)} %get-tuple-element.94), channel_id=1, source_target_pairs={{1,0},{2,1},{3,2},{4,3},{5,4},{6,5},{7,6},{8,7},{9,8},{10,9},{11,1... | collective-permute-start | bytes 1568 | tf_op jit(solution)/shard_map/ppermute | solution.py:26
  121.8 1.9 collective-permute-start.5
  123.7 2.4 collective-permute-start.4
  126.4 4.0 %collective-permute-start.25 = (f32[2,8,1]{2,1,0:T(8,128)S(1)}, f32[2,8,1]{2,1,0:T(8,128)S(1)}, u32[]{:S(2)}, u32[]{:S(2)}) collective-permute-start(f32[2,8,1]{2,1,0:T(8,128)S(1)} %get-tuple-element.99), channel_id=1, source_target_pairs={{16,0},{32,16},{48,32},{64,48},{80,64},{96,80},{112,96},{128,112},... | collective-permute-start | bytes 200 | tf_op jit(solution)/shard_map/ppermute | solution.py:26
  130.5 1.9 collective-permute-start.24
  132.4 3.9 %collective-permute-done.24 = f32[2,8,1]{2,1,0:T(8,128)S(1)} collective-permute-done((f32[2,8,1]{2,1,0:T(8,128)S(1)}, f32[2,8,1]{2,1,0:T(8,128)S(1)}, u32[]{:S(2)}, u32[]{:S(2)}) %collective-permute-start.24) | collective-permute-done | bytes 96 | tf_op jit(solution)/shard_map/ppermute | solution.py:23
  136.5 2.3 collective-permute-start.27
  138.7 3.6 %collective-permute-start.26 = (f32[2,1,130]{2,1,0:T(1,128)S(1)}, f32[2,1,130]{2,1,0:T(1,128)S(1)}, u32[]{:S(2)}, u32[]{:S(2)}) collective-permute-start(f32[2,1,130]{2,1,0:T(1,128)S(1)} %get-tuple-element.88), channel_id=1, source_target_pairs={{0,1},{1,2},{2,3},{3,4},{4,5},{5,6},{6,7},{7,8},{8,9},{9,10},{10,1... | collective-permute-start | bytes 3128 | tf_op jit(solution)/shard_map/ppermute | solution.py:23
  143.6 2.1 copy.436
  145.9 5.9 %collective-permute-start.7 = (f32[3,32,2,132]{1,2,3,0:T(2,128)S(1)}, f32[3,32,2,132]{1,2,3,0:T(2,128)S(1)}, u32[]{:S(2)}, u32[]{:S(2)}) collective-permute-start(f32[3,32,2,132]{1,2,3,0:T(2,128)S(1)} %get-tuple-element.58), channel_id=1, source_target_pairs={{1,0},{2,1},{3,2},{4,3},{5,4},{6,5},{7,6},{8,7},{9,8},{10,9},{11,1... | collective-permute-start | bytes 304136 | tf_op jit(solution)/shard_map/ppermute | solution.py:26
  151.8 2.1 collective-permute-start.6
  154.1 4.0 %collective-permute-done.7 = f32[3,32,2,132]{1,2,3,0:T(2,128)S(1)} collective-permute-done((f32[3,32,2,132]{1,2,3,0:T(2,128)S(1)}, f32[3,32,2,132]{1,2,3,0:T(2,128)S(1)}, u32[]{:S(2)}, u32[]{:S(2)}) %collective-permute-start.7) | collective-permute-done | bytes 101408 | tf_op jit(solution)/shard_map/ppermute | solution.py:26
  158.0 8.4 %collective-permute-done.6 = f32[3,32,2,132]{1,2,3,0:T(2,128)S(1)} collective-permute-done((f32[3,32,2,132]{1,2,3,0:T(2,128)S(1)}, f32[3,32,2,132]{1,2,3,0:T(2,128)S(1)}, u32[]{:S(2)}, u32[]{:S(2)}) %collective-permute-start.6) | collective-permute-done | bytes 101408 | tf_op jit(solution)/shard_map/ppermute | solution.py:23
  169.4 2.3 bitcast_dynamic-update-slice_fusion.5
  174.3 2.0 bitcast_dynamic-update-slice_fusion.2
  176.3 2.0 bitcast_dynamic-update-slice_fusion.1
  178.3 2.0 bitcast_dynamic-update-slice_fusion
  180.3 2.9 collective-permute-start.13
  183.2 1.9 collective-permute-start.12
  185.8 3.7 %collective-permute-done.12 = f32[6,32,8,2]{1,2,3,0:T(8,128)S(1)} collective-permute-done((f32[6,32,8,2]{1,2,3,0:T(8,128)S(1)}, f32[6,32,8,2]{1,2,3,0:T(8,128)S(1)}, u32[]{:S(2)}, u32[]{:S(2)}) %collective-permute-start.12) | collective-permute-done | bytes 12320 | tf_op jit(solution)/shard_map/ppermute | solution.py:23
  190.7 1.9 collective-permute-start.15
  193.2 4.1 %collective-permute-start.14 = (f32[6,32,2,132]{3,1,2,0:T(8,128)S(1)}, f32[6,32,2,132]{3,1,2,0:T(8,128)}, u32[]{:S(2)}, u32[]{:S(2)}) collective-permute-start(f32[6,32,2,132]{3,1,2,0:T(8,128)S(1)} %copy.450), channel_id=1, source_target_pairs={{0,1},{1,2},{2,3},{3,4},{4,5},{5,6},{6,7},{7,8},{8,9},{9,10},{10,1... | collective-permute-start | bytes 608264 | tf_op jit(solution)/shard_map/ppermute | solution.py:23
  197.9 4.1 %collective-permute-done.15 = f32[6,32,2,132]{3,1,2,0:T(8,128)S(1)} collective-permute-done((f32[6,32,2,132]{3,1,2,0:T(8,128)S(1)}, f32[6,32,2,132]{3,1,2,0:T(8,128)S(1)}, u32[]{:S(2)}, u32[]{:S(2)}) %collective-permute-start.15) | collective-permute-done | bytes 202784 | tf_op jit(solution)/shard_map/ppermute | solution.py:26
  202.7 5.5 %collective-permute-done.14 = f32[6,32,2,132]{3,1,2,0:T(8,128)} collective-permute-done((f32[6,32,2,132]{3,1,2,0:T(8,128)S(1)}, f32[6,32,2,132]{3,1,2,0:T(8,128)}, u32[]{:S(2)}, u32[]{:S(2)}) %collective-permute-start.14) | collective-permute-done | bytes 202784 | tf_op jit(solution)/shard_map/ppermute | solution.py:23
  209.9 6.1 %select_maximum_fusion = f32[6,36,12,132]{1,2,3,0:T(8,128)S(1)} fusion(f32[6,32,2,132]{1,2,3,0:T(2,128)S(1)} %copy.453, f32[6,32,2,132]{1,2,3,0:T(2,128)S(1)} %copy.452, f32[6,32,8,2]{1,2,3,0:T(8,128)S(1)} %collective-permute-done.13, f32[6,32,8,128]{1,2,3,0:T(8,128)} %copy-done.3, f32[6,32,8,2]{1,2,3,0:T(8,128)S(1)} %collective-permute-done.12), kind=kLoop, calls=%fused_computation.2 | loop fusion | flops 4105728 | bytes 2585088 | tf_op jit(solution)/shard_map/concatenate | solution.py:27
  218.7 2.4 fusion.82
  223.0 6.6 %fusion.68 = f32[1,32,8,128]{1,2,3,0:T(8,128)} fusion(f32[32,8,128]{0,1,2:T(8,128)} %fusion.144, f32[36,12,132]{0,1,2:T(8,128)S(1)} %get-tuple-element.32, f32[36,12,132]{0,1,2:T(8,128)} %get-tuple-element.33, f32[36,12,132]{0,1,2:T(8,128)} %copy-done.2, f32[32,8,128]{0,1,2:T(8,128)S(1)} %copy.423), kind=kLoop, calls=%fused_computation.131 | loop fusion | flops 655360 | bytes 1966080 | tf_op jit(solution)/shard_map/stack | solution.py:67
  230.8 5.9 %select_reduce_fusion = (f32[8,128]{0,1:T(8,128)}, f32[32,8,128]{0,1,2:T(8,128)}) fusion(s32[8,128]{0,1:T(8,128)S(1)} %copy.443, f32[32,8,128]{0,1,2:T(8,128)} %get-tuple-element.25, f32[36,12,132]{0,1,2:T(8,128)} %get-tuple-element.31, f32[36,12,132]{0,1,2:T(8,128)S(1)} %get-tuple-element.32, f32[36,12,132]{0,1,2:T(8,128)S(1)} %get-tuple-element.34, ...), kind=kLoop, calls=%fused_computation.285 | loop fusion | flops 752640 | bytes 1974272 | tf_op jit(solution)/shard_map/reduce_sum | solution.py:98
  239.7 1.9 collective-permute-start.29
  241.6 4.5 %collective-permute-start.28 = (f32[8,1]{1,0:T(8,128)S(1)}, f32[8,1]{1,0:T(8,128)S(1)}, u32[]{:S(2)}, u32[]{:S(2)}) collective-permute-start(f32[8,1]{1,0:T(8,128)S(1)} %get-tuple-element.101), channel_id=1, source_target_pairs={{16,0},{32,16},{48,32},{64,48},{80,64},{96,80},{112,96},{128,112},... | collective-permute-start | bytes 104 | tf_op jit(solution)/shard_map/ppermute | solution.py:26
  247.5 1.9 collective-permute-start.31
  249.4 7.5 %collective-permute-start.30 = (f32[1,130]{1,0:T(1,128)S(1)}, f32[1,130]{1,0:T(1,128)S(1)}, u32[]{:S(2)}, u32[]{:S(2)}) collective-permute-start(f32[1,130]{1,0:T(1,128)S(1)} %get-tuple-element.92), channel_id=1, source_target_pairs={{1,0},{2,1},{3,2},{4,3},{5,4},{6,5},{7,6},{8,7},{9,8},{10,9},{11,1... | collective-permute-start | bytes 1568 | tf_op jit(solution)/shard_map/ppermute | solution.py:26
  257.7 3.9 %collective-permute-start.17 = (f32[3,32,8,2]{3,2,1,0:T(8,128)S(1)}, f32[3,32,8,2]{3,2,1,0:T(8,128)S(1)}, u32[]{:S(2)}, u32[]{:S(2)}) collective-permute-start(f32[3,32,8,2]{3,2,1,0:T(8,128)S(1)} %get-tuple-element.77), channel_id=1, source_target_pairs={{16,0},{32,16},{48,32},{64,48},{80,64},{96,80},{112,96},{128,112},... | collective-permute-start | bytes 18440 | tf_op jit(solution)/shard_map/ppermute | solution.py:26
  261.6 1.9 collective-permute-start.16
  265.0 2.0 collective-permute-done.17
  266.9 4.7 %collective-permute-done.16 = f32[3,32,8,2]{3,2,1,0:T(8,128)S(1)} collective-permute-done((f32[3,32,8,2]{3,2,1,0:T(8,128)S(1)}, f32[3,32,8,2]{3,2,1,0:T(8,128)S(1)}, u32[]{:S(2)}, u32[]{:S(2)}) %collective-permute-start.16) | collective-permute-done | bytes 6176 | tf_op jit(solution)/shard_map/ppermute | solution.py:23
  273.3 1.9 collective-permute-start.19
  275.2 4.2 %collective-permute-start.18 = (f32[3,32,2,132]{1,2,3,0:T(2,128)S(1)}, f32[3,32,2,132]{1,2,3,0:T(2,128)S(1)}, u32[]{:S(2)}, u32[]{:S(2)}) collective-permute-start(f32[3,32,2,132]{1,2,3,0:T(2,128)S(1)} %get-tuple-element.55), channel_id=1, source_target_pairs={{0,1},{1,2},{2,3},{3,4},{4,5},{5,6},{6,7},{7,8},{8,9},{9,10},{10,1... | collective-permute-start | bytes 304136 | tf_op jit(solution)/shard_map/ppermute | solution.py:23
  280.0 6.0 %collective-permute-done.19 = f32[3,32,2,132]{1,2,3,0:T(2,128)S(1)} collective-permute-done((f32[3,32,2,132]{1,2,3,0:T(2,128)S(1)}, f32[3,32,2,132]{1,2,3,0:T(2,128)S(1)}, u32[]{:S(2)}, u32[]{:S(2)}) %collective-permute-start.19) | collective-permute-done | bytes 101408 | tf_op jit(solution)/shard_map/ppermute | solution.py:26
  286.0 5.5 %collective-permute-done.18 = f32[3,32,2,132]{1,2,3,0:T(2,128)S(1)} collective-permute-done((f32[3,32,2,132]{1,2,3,0:T(2,128)S(1)}, f32[3,32,2,132]{1,2,3,0:T(2,128)S(1)}, u32[]{:S(2)}, u32[]{:S(2)}) %collective-permute-start.18) | collective-permute-done | bytes 101408 | tf_op jit(solution)/shard_map/ppermute | solution.py:23
  294.4 2.2 fusion.26
  296.6 2.3 fusion.10
  304.6 5.6 %fusion.16 = (f32[1,32,8,128]{1,2,3,0:T(8,128)}, f32[1,32,8,128]{1,2,3,0:T(8,128)}) fusion(f32[32,8,128]{0,1,2:T(8,128)} %get-tuple-element.15, f32[36,12,132]{0,1,2:T(8,128)} %copy-done, f32[36,12,132]{0,1,2:T(8,128)S(1)} %get-tuple-element.44, f32[32,8,128]{0,1,2:T(8,128)S(1)} %copy.440, f32[32,8,128]{0,1,2:T(8,128)S(1)} %copy-done.17, ...), kind=kLoop, calls=%fused_computation.55 | loop fusion | flops 884736 | bytes 2621440 | tf_op jit(solution)/shard_map/stack | solution.py:85
  (205 shorter events, 69.3 us)
Async XLA Ops:
  2.3 6.5 %copy-start.33 = (f32[3,8,128]{2,1,0:T(8,128)S(1)}, f32[3,8,128]{2,1,0:T(8,128)}, u32[]{:S(2)}) copy-start(f32[3,8,128]{2,1,0:T(8,128)} %param.12) | copy-start | bytes 36868
  3.3 35.9 %collective-permute-start.1 = (f32[6,32,8,2]{1,2,3,0:T(8,128)}, f32[6,32,8,2]{1,2,3,0:T(8,128)}, u32[]{:S(2)}, u32[]{:S(2)}) collective-permute-start(f32[6,32,8,2]{1,2,3,0:T(8,128)} %copy.475), channel_id=1, source_target_pairs={{16,0},{32,16},{48,32},{64,48},{80,64},{96,80},{112,96},{128,112},... | collective-permute-start | bytes 36872 | tf_op jit(solution)/shard_map/ppermute | solution.py:26
  5.9 9.5 %copy-start.4 = (f32[9,32,8,128]{3,2,1,0:T(8,128)S(1)}, f32[9,32,8,128]{3,2,1,0:T(8,128)}, u32[]{:S(2)}) copy-start(f32[9,32,8,128]{3,2,1,0:T(8,128)} %param.8) | copy-start | bytes 3538948
  6.9 33.4 %collective-permute-start = (f32[6,32,8,2]{1,2,3,0:T(8,128)}, f32[6,32,8,2]{1,2,3,0:T(8,128)}, u32[]{:S(2)}, u32[]{:S(2)}) collective-permute-start(f32[6,32,8,2]{1,2,3,0:T(8,128)} %copy.473), channel_id=1, source_target_pairs={{0,16},{16,32},{32,48},{48,64},{64,80},{80,96},{96,112},{112,128},... | collective-permute-start | bytes 36872 | tf_op jit(solution)/shard_map/ppermute | solution.py:23
  8.9 9.3 %collective-permute-start.9 = (f32[2,8,1]{2,1,0:T(8,128)S(1)}, f32[2,8,1]{2,1,0:T(8,128)S(1)}, u32[]{:S(2)}, u32[]{:S(2)}) collective-permute-start(f32[2,8,1]{2,1,0:T(8,128)S(1)} %get-tuple-element.97), channel_id=1, source_target_pairs={{16,0},{32,16},{48,32},{64,48},{80,64},{96,80},{112,96},{128,112},... | collective-permute-start | bytes 200 | tf_op jit(solution)/shard_map/ppermute | solution.py:26
  13.4 5.9 %collective-permute-start.8 = (f32[2,8,1]{2,1,0:T(8,128)S(1)}, f32[2,8,1]{2,1,0:T(8,128)S(1)}, u32[]{:S(2)}, u32[]{:S(2)}) collective-permute-start(f32[2,8,1]{2,1,0:T(8,128)S(1)} %get-tuple-element.96), channel_id=1, source_target_pairs={{0,16},{16,32},{32,48},{48,64},{64,80},{80,96},{96,112},{112,128},... | collective-permute-start | bytes 200 | tf_op jit(solution)/shard_map/ppermute | solution.py:23
  16.6 13.5 %copy-start.32 = (f32[32,8,128]{2,1,0:T(8,128)S(1)}, f32[32,8,128]{2,1,0:T(8,128)}, u32[]{:S(2)}) copy-start(f32[32,8,128]{2,1,0:T(8,128)} %param.9) | copy-start | bytes 393220
  17.7 13.5 %copy-start.47 = (s32[8,128]{1,0:T(8,128)S(1)}, s32[8,128]{1,0:T(8,128)}, u32[]{:S(2)}) copy-start(s32[8,128]{1,0:T(8,128)} %param.14) | copy-start | bytes 12292
  19.4 19.1 %collective-permute-start.11 = (f32[2,1,130]{2,1,0:T(1,128)S(1)}, f32[2,1,130]{2,1,0:T(1,128)S(1)}, u32[]{:S(2)}, u32[]{:S(2)}) collective-permute-start(f32[2,1,130]{2,1,0:T(1,128)S(1)} %get-tuple-element.91), channel_id=1, source_target_pairs={{1,0},{2,1},{3,2},{4,3},{5,4},{6,5},{7,6},{8,7},{9,8},{10,9},{11,1... | collective-permute-start | bytes 3128 | tf_op jit(solution)/shard_map/ppermute | solution.py:26
  27.2 11.2 %collective-permute-start.10 = (f32[2,1,130]{2,1,0:T(1,128)S(1)}, f32[2,1,130]{2,1,0:T(1,128)S(1)}, u32[]{:S(2)}, u32[]{:S(2)}) collective-permute-start(f32[2,1,130]{2,1,0:T(1,128)S(1)} %get-tuple-element.90), channel_id=1, source_target_pairs={{0,1},{1,2},{2,3},{3,4},{4,5},{5,6},{6,7},{7,8},{8,9},{9,10},{10,1... | collective-permute-start | bytes 3128 | tf_op jit(solution)/shard_map/ppermute | solution.py:23
  42.3 23.4 %copy-start.7 = (f32[6,32,8,2]{3,1,2,0:T(8,128)S(1)}, f32[6,32,8,2]{3,1,2,0:T(8,128)}, u32[]{:S(2)}) copy-start(f32[6,32,8,2]{3,1,2,0:T(8,128)} %copy.427) | copy-start | bytes 36868
  43.8 14.2 %collective-permute-start.3 = (f32[6,32,2,132]{3,1,2,0:T(8,128)S(1)}, f32[6,32,2,132]{3,1,2,0:T(8,128)S(1)}, u32[]{:S(2)}, u32[]{:S(2)}) collective-permute-start(f32[6,32,2,132]{3,1,2,0:T(8,128)S(1)} %get-tuple-element.54), channel_id=1, source_target_pairs={{1,0},{2,1},{3,2},{4,3},{5,4},{6,5},{7,6},{8,7},{9,8},{10,9},{11,1... | collective-permute-start | bytes 608264 | tf_op jit(solution)/shard_map/ppermute | solution.py:26
  51.3 14.4 %collective-permute-start.2 = (f32[6,32,2,132]{3,1,2,0:T(8,128)S(1)}, f32[6,32,2,132]{3,1,2,0:T(8,128)S(1)}, u32[]{:S(2)}, u32[]{:S(2)}) collective-permute-start(f32[6,32,2,132]{3,1,2,0:T(8,128)S(1)} %get-tuple-element.53), channel_id=1, source_target_pairs={{0,1},{1,2},{2,3},{3,4},{4,5},{5,6},{6,7},{7,8},{8,9},{9,10},{10,1... | collective-permute-start | bytes 608264 | tf_op jit(solution)/shard_map/ppermute | solution.py:23
  74.7 6.1 %copy-start.26 = (f32[1,32,8,128]{1,2,3,0:T(8,128)S(1)}, f32[1,32,8,128]{1,2,3,0:T(8,128)}, u32[]{:S(2)}) copy-start(f32[1,32,8,128]{1,2,3,0:T(8,128)} %copy.478) | copy-start | bytes 393220
  80.8 3.3 %copy-start.1 = (f32[36,12,132]{0,1,2:T(8,128)}, f32[36,12,132]{0,1,2:T(8,128)S(1)}, u32[]{:S(2)}) copy-start(f32[36,12,132]{0,1,2:T(8,128)S(1)} %get-tuple-element.40) | copy-start | bytes 684292
  101.7 6.5 %collective-permute-start.20 = (f32[8,1]{1,0:T(8,128)S(1)}, f32[8,1]{1,0:T(8,128)S(1)}, u32[]{:S(2)}, u32[]{:S(2)}) collective-permute-start(f32[8,1]{1,0:T(8,128)S(1)} %get-tuple-element.102), channel_id=1, source_target_pairs={{16,0},{32,16},{48,32},{64,48},{80,64},{96,80},{112,96},{128,112},... | collective-permute-start | bytes 104 | tf_op jit(solution)/shard_map/ppermute | solution.py:26
  106.1 20.2 %copy-start.34 = (f32[3,8,128]{2,1,0:T(8,128)S(1)}, f32[3,8,128]{2,1,0:T(8,128)}, u32[]{:S(2)}) copy-start(f32[3,8,128]{2,1,0:T(8,128)} %param.12) | copy-start | bytes 36868
  106.1 20.2 %copy-start.35 = (s32[8,128]{1,0:T(8,128)S(1)}, s32[8,128]{1,0:T(8,128)}, u32[]{:S(2)}) copy-start(s32[8,128]{1,0:T(8,128)} %param.15) | copy-start | bytes 12292
  106.1 20.2 %copy-start.40 = (f32[2,8,128]{2,1,0:T(8,128)S(1)}, f32[2,8,128]{2,1,0:T(8,128)}, u32[]{:S(2)}) copy-start(f32[2,8,128]{2,1,0:T(8,128)} %fusion.174) | copy-start | bytes 24580
  106.1 20.2 %copy-start.41 = (f32[8,128]{1,0:T(8,128)S(1)}, f32[8,128]{1,0:T(8,128)}, u32[]{:S(2)}) copy-start(f32[8,128]{1,0:T(8,128)} %param.13) | copy-start | bytes 12292
  106.1 6.0 %collective-permute-start.21 = (f32[8,1]{1,0:T(8,128)S(1)}, f32[8,1]{1,0:T(8,128)S(1)}, u32[]{:S(2)}, u32[]{:S(2)}) collective-permute-start(f32[8,1]{1,0:T(8,128)S(1)} %get-tuple-element.103), channel_id=1, source_target_pairs={{0,16},{16,32},{32,48},{48,64},{64,80},{80,96},{96,112},{112,128},... | collective-permute-start | bytes 104 | tf_op jit(solution)/shard_map/ppermute | solution.py:23
  112.1 14.1 %collective-permute-start.23 = (f32[1,130]{1,0:T(1,128)S(1)}, f32[1,130]{1,0:T(1,128)S(1)}, u32[]{:S(2)}, u32[]{:S(2)}) collective-permute-start(f32[1,130]{1,0:T(1,128)S(1)} %get-tuple-element.95), channel_id=1, source_target_pairs={{0,1},{1,2},{2,3},{3,4},{4,5},{5,6},{6,7},{7,8},{8,9},{9,10},{10,1... | collective-permute-start | bytes 1568 | tf_op jit(solution)/shard_map/ppermute | solution.py:23
  114.1 12.2 %collective-permute-start.22 = (f32[1,130]{1,0:T(1,128)S(1)}, f32[1,130]{1,0:T(1,128)S(1)}, u32[]{:S(2)}, u32[]{:S(2)}) collective-permute-start(f32[1,130]{1,0:T(1,128)S(1)} %get-tuple-element.94), channel_id=1, source_target_pairs={{1,0},{2,1},{3,2},{4,3},{5,4},{6,5},{7,6},{8,7},{9,8},{10,9},{11,1... | collective-permute-start | bytes 1568 | tf_op jit(solution)/shard_map/ppermute | solution.py:26
  121.8 20.5 %collective-permute-start.5 = (f32[3,32,8,2]{3,2,1,0:T(8,128)S(1)}, f32[3,32,8,2]{3,2,1,0:T(8,128)S(1)}, u32[]{:S(2)}, u32[]{:S(2)}) collective-permute-start(f32[3,32,8,2]{3,2,1,0:T(8,128)S(1)} %get-tuple-element.79), channel_id=1, source_target_pairs={{16,0},{32,16},{48,32},{64,48},{80,64},{96,80},{112,96},{128,112},... | collective-permute-start | bytes 18440 | tf_op jit(solution)/shard_map/ppermute | solution.py:26
  123.7 18.6 %collective-permute-start.4 = (f32[3,32,8,2]{3,2,1,0:T(8,128)S(1)}, f32[3,32,8,2]{3,2,1,0:T(8,128)S(1)}, u32[]{:S(2)}, u32[]{:S(2)}) collective-permute-start(f32[3,32,8,2]{3,2,1,0:T(8,128)S(1)} %get-tuple-element.78), channel_id=1, source_target_pairs={{0,16},{16,32},{32,48},{48,64},{64,80},{80,96},{96,112},{112,128},... | collective-permute-start | bytes 18440 | tf_op jit(solution)/shard_map/ppermute | solution.py:23
  126.4 6.0 %collective-permute-start.25 = (f32[2,8,1]{2,1,0:T(8,128)S(1)}, f32[2,8,1]{2,1,0:T(8,128)S(1)}, u32[]{:S(2)}, u32[]{:S(2)}) collective-permute-start(f32[2,8,1]{2,1,0:T(8,128)S(1)} %get-tuple-element.99), channel_id=1, source_target_pairs={{16,0},{32,16},{48,32},{64,48},{80,64},{96,80},{112,96},{128,112},... | collective-permute-start | bytes 200 | tf_op jit(solution)/shard_map/ppermute | solution.py:26
  130.5 5.9 %collective-permute-start.24 = (f32[2,8,1]{2,1,0:T(8,128)S(1)}, f32[2,8,1]{2,1,0:T(8,128)S(1)}, u32[]{:S(2)}, u32[]{:S(2)}) collective-permute-start(f32[2,8,1]{2,1,0:T(8,128)S(1)} %get-tuple-element.98), channel_id=1, source_target_pairs={{0,16},{16,32},{32,48},{48,64},{64,80},{80,96},{96,112},{112,128},... | collective-permute-start | bytes 200 | tf_op jit(solution)/shard_map/ppermute | solution.py:23
  136.5 17.5 %collective-permute-start.27 = (f32[2,1,130]{2,1,0:T(1,128)S(1)}, f32[2,1,130]{2,1,0:T(1,128)S(1)}, u32[]{:S(2)}, u32[]{:S(2)}) collective-permute-start(f32[2,1,130]{2,1,0:T(1,128)S(1)} %get-tuple-element.89), channel_id=1, source_target_pairs={{1,0},{2,1},{3,2},{4,3},{5,4},{6,5},{7,6},{8,7},{9,8},{10,9},{11,1... | collective-permute-start | bytes 3128 | tf_op jit(solution)/shard_map/ppermute | solution.py:26
  138.7 15.2 %collective-permute-start.26 = (f32[2,1,130]{2,1,0:T(1,128)S(1)}, f32[2,1,130]{2,1,0:T(1,128)S(1)}, u32[]{:S(2)}, u32[]{:S(2)}) collective-permute-start(f32[2,1,130]{2,1,0:T(1,128)S(1)} %get-tuple-element.88), channel_id=1, source_target_pairs={{0,1},{1,2},{2,3},{3,4},{4,5},{5,6},{6,7},{7,8},{8,9},{9,10},{10,1... | collective-permute-start | bytes 3128 | tf_op jit(solution)/shard_map/ppermute | solution.py:23
  145.9 12.1 %collective-permute-start.7 = (f32[3,32,2,132]{1,2,3,0:T(2,128)S(1)}, f32[3,32,2,132]{1,2,3,0:T(2,128)S(1)}, u32[]{:S(2)}, u32[]{:S(2)}) collective-permute-start(f32[3,32,2,132]{1,2,3,0:T(2,128)S(1)} %get-tuple-element.58), channel_id=1, source_target_pairs={{1,0},{2,1},{3,2},{4,3},{5,4},{6,5},{7,6},{8,7},{9,8},{10,9},{11,1... | collective-permute-start | bytes 304136 | tf_op jit(solution)/shard_map/ppermute | solution.py:26
  151.8 14.5 %collective-permute-start.6 = (f32[3,32,2,132]{1,2,3,0:T(2,128)S(1)}, f32[3,32,2,132]{1,2,3,0:T(2,128)S(1)}, u32[]{:S(2)}, u32[]{:S(2)}) collective-permute-start(f32[3,32,2,132]{1,2,3,0:T(2,128)S(1)} %get-tuple-element.57), channel_id=1, source_target_pairs={{0,1},{1,2},{2,3},{3,4},{4,5},{5,6},{6,7},{7,8},{8,9},{9,10},{10,1... | collective-permute-start | bytes 304136 | tf_op jit(solution)/shard_map/ppermute | solution.py:23
  154.0 14.2 %copy-start.45 = (f32[2,1,130]{2,1,0:T(1,128)}, f32[2,1,130]{2,1,0:T(1,128)S(1)}, u32[]{:S(2)}) copy-start(f32[2,1,130]{2,1,0:T(1,128)S(1)} %collective-permute-done.26) | copy-start | bytes 3124
  169.4 2.3 copy-start.12
  178.3 6.8 %copy-start.46 = (f32[2,1,130]{2,1,0:T(1,128)S(1)}, f32[2,1,130]{2,1,0:T(1,128)}, u32[]{:S(2)}) copy-start(f32[2,1,130]{2,1,0:T(1,128)} %copy-done.45) | copy-start | bytes 3124
  180.3 9.8 %copy-start.3 = (f32[6,32,8,128]{1,2,3,0:T(8,128)}, f32[6,32,8,128]{1,2,3,0:T(8,128)S(1)}, u32[]{:S(2)}) copy-start(f32[6,32,8,128]{1,2,3,0:T(8,128)S(1)} %get-tuple-element.14) | copy-start | bytes 2359300
  180.3 5.5 %collective-permute-start.13 = (f32[6,32,8,2]{1,2,3,0:T(8,128)S(1)}, f32[6,32,8,2]{1,2,3,0:T(8,128)S(1)}, u32[]{:S(2)}, u32[]{:S(2)}) collective-permute-start(f32[6,32,8,2]{1,2,3,0:T(8,128)S(1)} %get-tuple-element.52), channel_id=1, source_target_pairs={{16,0},{32,16},{48,32},{64,48},{80,64},{96,80},{112,96},{128,112},... | collective-permute-start | bytes 36872 | tf_op jit(solution)/shard_map/ppermute | solution.py:26
  183.2 6.3 %collective-permute-start.12 = (f32[6,32,8,2]{1,2,3,0:T(8,128)S(1)}, f32[6,32,8,2]{1,2,3,0:T(8,128)S(1)}, u32[]{:S(2)}, u32[]{:S(2)}) collective-permute-start(f32[6,32,8,2]{1,2,3,0:T(8,128)S(1)} %get-tuple-element.51), channel_id=1, source_target_pairs={{0,16},{16,32},{32,48},{48,64},{64,80},{80,96},{96,112},{112,128},... | collective-permute-start | bytes 36872 | tf_op jit(solution)/shard_map/ppermute | solution.py:23
  190.7 11.4 %collective-permute-start.15 = (f32[6,32,2,132]{3,1,2,0:T(8,128)S(1)}, f32[6,32,2,132]{3,1,2,0:T(8,128)S(1)}, u32[]{:S(2)}, u32[]{:S(2)}) collective-permute-start(f32[6,32,2,132]{3,1,2,0:T(8,128)S(1)} %copy.451), channel_id=1, source_target_pairs={{1,0},{2,1},{3,2},{4,3},{5,4},{6,5},{7,6},{8,7},{9,8},{10,9},{11,1... | collective-permute-start | bytes 608264 | tf_op jit(solution)/shard_map/ppermute | solution.py:26
  193.2 15.1 %collective-permute-start.14 = (f32[6,32,2,132]{3,1,2,0:T(8,128)S(1)}, f32[6,32,2,132]{3,1,2,0:T(8,128)}, u32[]{:S(2)}, u32[]{:S(2)}) collective-permute-start(f32[6,32,2,132]{3,1,2,0:T(8,128)S(1)} %copy.450), channel_id=1, source_target_pairs={{0,1},{1,2},{2,3},{3,4},{4,5},{5,6},{6,7},{7,8},{8,9},{9,10},{10,1... | collective-permute-start | bytes 608264 | tf_op jit(solution)/shard_map/ppermute | solution.py:23
  216.0 2.7 copy-start.16
  238.6 25.6 %copy-start.39 = (f32[2,8,128]{2,1,0:T(8,128)S(1)}, f32[2,8,128]{2,1,0:T(8,128)}, u32[]{:S(2)}) copy-start(f32[2,8,128]{2,1,0:T(8,128)} %fusion.169) | copy-start | bytes 24580
  238.7 25.6 %copy-start.42 = (f32[8,128]{1,0:T(8,128)S(1)}, f32[8,128]{1,0:T(8,128)}, u32[]{:S(2)}) copy-start(f32[8,128]{1,0:T(8,128)} %param.13) | copy-start | bytes 12292
  239.7 6.5 %collective-permute-start.29 = (f32[8,1]{1,0:T(8,128)S(1)}, f32[8,1]{1,0:T(8,128)S(1)}, u32[]{:S(2)}, u32[]{:S(2)}) collective-permute-start(f32[8,1]{1,0:T(8,128)S(1)} %get-tuple-element.100), channel_id=1, source_target_pairs={{0,16},{16,32},{32,48},{48,64},{64,80},{80,96},{96,112},{112,128},... | collective-permute-start | bytes 104 | tf_op jit(solution)/shard_map/ppermute | solution.py:23
  241.6 5.9 %collective-permute-start.28 = (f32[8,1]{1,0:T(8,128)S(1)}, f32[8,1]{1,0:T(8,128)S(1)}, u32[]{:S(2)}, u32[]{:S(2)}) collective-permute-start(f32[8,1]{1,0:T(8,128)S(1)} %get-tuple-element.101), channel_id=1, source_target_pairs={{16,0},{32,16},{48,32},{64,48},{80,64},{96,80},{112,96},{128,112},... | collective-permute-start | bytes 104 | tf_op jit(solution)/shard_map/ppermute | solution.py:26
  247.5 16.7 %collective-permute-start.31 = (f32[1,130]{1,0:T(1,128)S(1)}, f32[1,130]{1,0:T(1,128)S(1)}, u32[]{:S(2)}, u32[]{:S(2)}) collective-permute-start(f32[1,130]{1,0:T(1,128)S(1)} %get-tuple-element.93), channel_id=1, source_target_pairs={{0,1},{1,2},{2,3},{3,4},{4,5},{5,6},{6,7},{7,8},{8,9},{9,10},{10,1... | collective-permute-start | bytes 1568 | tf_op jit(solution)/shard_map/ppermute | solution.py:23
  249.4 14.8 %collective-permute-start.30 = (f32[1,130]{1,0:T(1,128)S(1)}, f32[1,130]{1,0:T(1,128)S(1)}, u32[]{:S(2)}, u32[]{:S(2)}) collective-permute-start(f32[1,130]{1,0:T(1,128)S(1)} %get-tuple-element.92), channel_id=1, source_target_pairs={{1,0},{2,1},{3,2},{4,3},{5,4},{6,5},{7,6},{8,7},{9,8},{10,9},{11,1... | collective-permute-start | bytes 1568 | tf_op jit(solution)/shard_map/ppermute | solution.py:26
  257.7 9.3 %collective-permute-start.17 = (f32[3,32,8,2]{3,2,1,0:T(8,128)S(1)}, f32[3,32,8,2]{3,2,1,0:T(8,128)S(1)}, u32[]{:S(2)}, u32[]{:S(2)}) collective-permute-start(f32[3,32,8,2]{3,2,1,0:T(8,128)S(1)} %get-tuple-element.77), channel_id=1, source_target_pairs={{16,0},{32,16},{48,32},{64,48},{80,64},{96,80},{112,96},{128,112},... | collective-permute-start | bytes 18440 | tf_op jit(solution)/shard_map/ppermute | solution.py:26
  261.6 10.0 %collective-permute-start.16 = (f32[3,32,8,2]{3,2,1,0:T(8,128)S(1)}, f32[3,32,8,2]{3,2,1,0:T(8,128)S(1)}, u32[]{:S(2)}, u32[]{:S(2)}) collective-permute-start(f32[3,32,8,2]{3,2,1,0:T(8,128)S(1)} %get-tuple-element.76), channel_id=1, source_target_pairs={{0,16},{16,32},{32,48},{48,64},{64,80},{80,96},{96,112},{112,128},... | collective-permute-start | bytes 18440 | tf_op jit(solution)/shard_map/ppermute | solution.py:23
  273.0 6.4 %copy-start.43 = (f32[1,8,128]{2,1,0:T(8,128)S(1)}, f32[1,8,128]{2,1,0:T(8,128)}, u32[]{:S(2)}) copy-start(f32[1,8,128]{2,1,0:T(8,128)} %get-tuple-element.86) | copy-start | bytes 12292
  273.0 6.4 %copy-start.44 = (f32[1,8,128]{2,1,0:T(8,128)S(1)}, f32[1,8,128]{2,1,0:T(8,128)}, u32[]{:S(2)}) copy-start(f32[1,8,128]{2,1,0:T(8,128)} %get-tuple-element.87) | copy-start | bytes 12292
  273.3 12.8 %collective-permute-start.19 = (f32[3,32,2,132]{1,2,3,0:T(2,128)S(1)}, f32[3,32,2,132]{1,2,3,0:T(2,128)S(1)}, u32[]{:S(2)}, u32[]{:S(2)}) collective-permute-start(f32[3,32,2,132]{1,2,3,0:T(2,128)S(1)} %get-tuple-element.56), channel_id=1, source_target_pairs={{1,0},{2,1},{3,2},{4,3},{5,4},{6,5},{7,6},{8,7},{9,8},{10,9},{11,1... | collective-permute-start | bytes 304136 | tf_op jit(solution)/shard_map/ppermute | solution.py:26
  275.2 16.4 %collective-permute-start.18 = (f32[3,32,2,132]{1,2,3,0:T(2,128)S(1)}, f32[3,32,2,132]{1,2,3,0:T(2,128)S(1)}, u32[]{:S(2)}, u32[]{:S(2)}) collective-permute-start(f32[3,32,2,132]{1,2,3,0:T(2,128)S(1)} %get-tuple-element.55), channel_id=1, source_target_pairs={{0,1},{1,2},{2,3},{3,4},{4,5},{5,6},{6,7},{7,8},{8,9},{9,10},{10,1... | collective-permute-start | bytes 304136 | tf_op jit(solution)/shard_map/ppermute | solution.py:23
  293.6 3.0 copy-start
  294.4 2.2 copy-start.9
  294.4 2.2 copy-start.22
  294.4 2.2 copy-start.28
  296.6 2.3 copy-start.6
  296.6 2.3 copy-start.11
  296.6 2.3 copy-start.13
  296.6 2.3 copy-start.15
  296.6 2.3 copy-start.24
  300.2 4.4 %copy-start.17 = (f32[32,8,128]{0,1,2:T(8,128)S(1)}, f32[32,8,128]{0,1,2:T(8,128)}, u32[]{:S(2)}) copy-start(f32[32,8,128]{0,1,2:T(8,128)} %get-tuple-element.19) | copy-start | bytes 393220
  310.3 2.5 copy-start.23
  310.3 4.1 %copy-start.27 = (f32[1,32,8,128]{3,2,1,0:T(8,128)S(1)}, f32[1,32,8,128]{3,2,1,0:T(8,128)}, u32[]{:S(2)}) copy-start(f32[1,32,8,128]{3,2,1,0:T(8,128)} %copy.468) | copy-start | bytes 393220
  (17 other events, 20.9 us)
where the time goes:
time: 323 us; the launch traced here: 317 us
  starting transfers between devices  109 us (34%)
  other arithmetic  71.1 us (22%)
  local copies, waits for them, and re-layouts  69.7 us (22%)
  waiting for transfers between devices  65.3 us (20%)
    ppermute x16, starting transfers between devices, extended(): lax.ppermute(lax.slice_in_dim(block, 0, width, axis=dim), axis, backward)  71.2 us
    ppermute x16, waiting for transfers between devices, extended(): lax.ppermute(lax.slice_in_dim(block, block.shape[dim] - width, None, axis...  44.4 us
    ppermute x16, starting transfers between devices, extended(): lax.ppermute(lax.slice_in_dim(block, block.shape[dim] - width, None, axis...  38.1 us
    unnamed x120, local copies, waits for them, and re-layouts  23 us
    ppermute x16, waiting for transfers between devices, extended(): lax.ppermute(lax.slice_in_dim(block, 0, width, axis=dim), axis, backward)  20.9 us
    concatenate x8, other arithmetic, extended(): block = jnp.concatenate([low, block, high], axis=dim)  13.6 us
    concatenate x3, local copies, waits for them, and re-layouts, extended(): block = jnp.concatenate([low, block, high], axis=dim)  9.84 us
    reduce_sum x2, other arithmetic, ocean_level(): seafloor = jnp.sum(vertical * onehot, axis=0)  9.15 us
  transfers between devices with their start and end apart: 32, of which 15 were waited for; matrix products, arithmetic and copies ran while one was open for 8% of the time, Pallas kernels for 0%

commit v1 on v0

v1 whole, which is shorter than its diff:
```python
import functools

import jax
import jax.numpy as jnp
from jax import lax
from jax.experimental import pallas as pl
from jax.experimental.pallas import tpu as pltpu
from jax.sharding import PartitionSpec as P

STEPS = 2
CHUNK = 8

near = 9.0 / 8.0
far = -1.0 / 24.0
courant = 0.3
ocean_rate = 0.3
uplift = 0.5
loading = 0.5
viscous = 0.1

YY, XY, YZ, XX, XZ, ZZ = range(6)
STRESS_SOURCE = (4, 6, 8, 3, 7, 5)


def turned(tile, shift, axis):
    return pltpu.roll(tile, shift % tile.shape[axis], axis)


def kernel(
    counts,
    fields_ref,
    lame_ref,
    shear_ref,
    buoy_ref,
    ocean_ref,
    depth_ref,
    index_ref,
    wet_ref,
    wave_out,
    ocean_out,
    stress_a,
    speed_a,
    lame,
    shear,
    buoy,
    ocean,
    depth,
    index,
    wet_i,
    stress_b,
    stress_c,
    speed_b,
    speed_c,
    halo_y,
    halo_o,
    pack,
    halo_x,
    edges,
    result_o,
    load_sem,
    out_sem,
    send_y,
    recv_y,
    send_o,
    recv_o,
    send_x,
    recv_x,
):
    count_x, count_y = counts
    at_x, at_y = lax.axis_index("gx"), lax.axis_index("gy")
    layers = fields_ref.shape[1]
    chunks = layers // CHUNK
    tile = (8, 128)

    has_y = (at_y < count_y - 1, at_y > 0)
    has_x = (at_x < count_x - 1, at_x > 0)
    to_y = ({"gy": jnp.minimum(at_y + 1, count_y - 1)}, {"gy": jnp.maximum(at_y - 1, 0)})
    to_x = ({"gx": jnp.minimum(at_x + 1, count_x - 1)}, {"gx": jnp.maximum(at_x - 1, 0)})

    loads = []

    def load(source, target):
        copy = pltpu.make_async_copy(source, target, load_sem.at[len(loads)])
        copy.start()
        loads.append(copy)

    for place, source in enumerate(STRESS_SOURCE):
        load(fields_ref.at[source], stress_a.at[place, pl.ds(2, layers)])
    load(ocean_ref, ocean)
    load(fields_ref.at[pl.ds(0, 3)], speed_a)
    load(buoy_ref, buoy)
    load(lame_ref, lame)
    load(shear_ref, shear)
    load(depth_ref, depth)
    load(index_ref, index)
    load(wet_ref, wet_i)

    none = jnp.zeros(tile, jnp.float32)
    for direction in range(2):
        @pl.when(jnp.logical_not(has_y[1 - direction]))
        def _():
            rows = slice(6, 8) if direction == 0 else slice(0, 2)

            def clear(z, carry):
                for number in range(2 * STEPS):
                    for field in range(3):
                        halo_y[number, field, z, rows, :] = jnp.zeros((2, 128), jnp.float32)
                return carry

            lax.fori_loop(0, layers, clear, 0)
            for number in range(2 * STEPS):
                for field in range(2):
                    row = slice(7, 8) if direction == 0 else slice(0, 1)
                    halo_o[number, field, row, :] = jnp.zeros((1, 128), jnp.float32)

        @pl.when(jnp.logical_not(has_x[1 - direction]))
        def _():
            for number in range(2 * STEPS):
                for place in range(4):
                    halo_x[number, direction, place] = none

    barrier = pltpu.get_barrier_semaphore()
    for has, to in ((has_y, to_y), (has_x, to_x)):
        for direction in range(2):

            @pl.when(has[direction])
            def _():
                pl.semaphore_signal(barrier, inc=1, device_id=to[direction])

    for stress in (stress_a, stress_b):
        for field in (YZ, XZ, ZZ):
            for z in (0, 1, layers + 2, layers + 3):
                stress[field, z] = none
    for speed in (speed_b, speed_c):
        for field in range(3):
            for z in (0, 1, layers + 2, layers + 3):
                speed[field, z] = none

    row_at = lax.broadcasted_iota(jnp.int32, tile, 0)
    lane_at = lax.broadcasted_iota(jnp.int32, tile, 1)
    group_at = lane_at // 4

    def rows_copy(number, source, direction, chunk):
        rows = pl.ds(6, 2) if direction == 0 else pl.ds(0, 2)
        return pltpu.make_async_remote_copy(
            source.at[pl.ds(0, 3), pl.ds(2 + chunk * CHUNK, CHUNK), rows, :],
            halo_y.at[number, :, pl.ds(chunk * CHUNK, CHUNK), rows, :],
            send_y.at[number, direction, chunk],
            recv_y.at[number, direction, chunk],
            device_id=to_y[direction],
        )

    def ocean_copy(number, direction):
        count = 2 if number % 2 == 0 else 1
        row = pl.ds(7, 1) if direction == 0 else pl.ds(0, 1)
        return pltpu.make_async_remote_copy(
            edges.at[number, pl.ds(0, count), row, :],
            halo_o.at[number, pl.ds(0, count), row, :],
            send_o.at[number, direction],
            recv_o.at[number, direction],
            device_id=to_y[direction],
        )

    def columns_copy(number, direction):
        return pltpu.make_async_remote_copy(
            pack.at[number],
            halo_x.at[number, direction],
            send_x.at[number, direction],
            recv_x.at[number, direction],
            device_id=to_x[direction],
        )

    def begin(make, has):
        for direction in range(2):

            @pl.when(has[direction])
            def _():
                make(direction).start()

    def arrive(make, has):
        for direction in range(2):

            @pl.when(has[1 - direction])
            def _():
                make(direction).wait_recv()

    def leave(make, has):
        for direction in range(2):

            @pl.when(has[direction])
            def _():
                make(direction).wait_send()

    def packed(held, tile_z, inner):
        return jnp.where(group_at == inner, turned(tile_z, 2 + 4 * inner, 1), held)

    def settle(held, part, chunk):
        moved = pltpu.roll(part, chunk * (4 * CHUNK), 1)
        return jnp.where(lane_at // (4 * CHUNK) == chunk, moved, held)

    def columns(number, place):
        low, high = halo_x[number, 0, place], halo_x[number, 1, place]
        return jnp.where(lane_at % 4 < 2, low, high)

    def chunk_columns(number, place, chunk):
        return pltpu.roll(columns(number, place), (128 - chunk * (4 * CHUNK)) % 128, 1)

    def unpacked(part, inner):
        return turned(part, -(2 + 4 * inner), 1)

    def shifted(tile_z, halo, axis, by):
        at, size = (row_at, 8) if axis == 0 else (lane_at, 128)
        from_halo = at >= size - by if by > 0 else at < -by
        return turned(jnp.where(from_halo, halo, tile_z), by, axis)

    def differ(tile_z, halo, axis, forward):
        before = shifted(tile_z, halo, axis, 1)
        after = shifted(tile_z, halo, axis, -1)
        if forward:
            after_two = shifted(tile_z, halo, axis, -2)
            return near * (after - tile_z) + far * (after_two - before)
        before_two = shifted(tile_z, halo, axis, 2)
        return near * (tile_z - before) + far * (after - before_two)

    def differ_z(ref, field, z, forward):
        at = [ref[field, z + 2 + k] for k in ((-1, 0, 1, 2) if forward else (-2, -1, 0, 1))]
        return near * (at[2] - at[1]) + far * (at[3] - at[0])

    def zero_pack():
        return (none, none, none)

    def pack_stress(stress, chunk, held):
        parts = [none, none, none]
        for inner in range(CHUNK):
            for place, field in enumerate((XX, XY, XZ)):
                parts[place] = packed(parts[place], stress[field, chunk * CHUNK + inner + 2], inner)
        return tuple(settle(h, p, chunk) for h, p in zip(held, parts))

    def finish_pack(number, held, extra):
        for place in range(3):
            pack[number, place] = held[place]
        last = none
        for place, item in enumerate(extra):
            last = packed(last, item, place)
        pack[number, 3] = last

    def velocity_stage(number, stress, speed_old, speed_new):
        arrive(functools.partial(columns_copy, number), has_x)

        def body(chunk, held):
            arrive(lambda d: rows_copy(number, stress, d, chunk), has_y)
            side = [chunk_columns(number, place, chunk) for place in range(3)]
            parts = [none, none, none]
            for inner in range(CHUNK):
                z = chunk * CHUNK + inner
                sxx, sxy, sxz = stress[XX, z + 2], stress[XY, z + 2], stress[XZ, z + 2]
                syy, syz = stress[YY, z + 2], stress[YZ, z + 2]
                hx = [unpacked(s, inner) for s in side]
                ax = (
                    differ(sxx, hx[0], 1, True)
                    + differ(sxy, halo_y[number, XY, z], 0, False)
                    + differ_z(stress, XZ, z, False)
                )
                ay = (
                    differ(sxy, hx[1], 1, False)
                    + differ(syy, halo_y[number, YY, z], 0, True)
                    + differ_z(stress, YZ, z, False)
                )
                az = (
                    differ(sxz, hx[2], 1, False)
                    + differ(syz, halo_y[number, YZ, z], 0, False)
                    + differ_z(stress, ZZ, z, True)
                )
                rate = courant * buoy[z]
                for field, push in enumerate((ax, ay, az)):
                    old = speed_old[field, z] if speed_old is speed_a else speed_old[field, z + 2]
                    new = old + rate * push
                    speed_new[field, z + 2] = new
                    parts[field] = packed(parts[field], new, inner)
            begin(lambda d: rows_copy(number + 1, speed_new, d, chunk), has_y)
            return tuple(settle(h, p, chunk) for h, p in zip(held, parts))

        return lax.fori_loop(0, chunks, body, zero_pack())

    def stress_stage(number, speed, stress_old, write, send):
        arrive(functools.partial(columns_copy, number), has_x)

        def body(chunk, held):
            arrive(lambda d: rows_copy(number, speed, d, chunk), has_y)
            side = [chunk_columns(number, place, chunk) for place in range(3)]
            parts = [none, none, none]
            for inner in range(CHUNK):
                z = chunk * CHUNK + inner
                vx, vy, vz = speed[0, z + 2], speed[1, z + 2], speed[2, z + 2]
                hx = [unpacked(s, inner) for s in side]
                hy = [halo_y[number, field, z] for field in range(3)]
                strain_x = differ(vx, hx[0], 1, False)
                strain_y = differ(vy, hy[1], 0, False)
                strain_z = differ_z(speed, 2, z, False)
                shear_xy = differ(vx, hy[0], 0, True) + differ(vy, hx[1], 1, True)
                shear_xz = differ_z(speed, 0, z, True) + differ(vz, hx[2], 1, True)
                shear_yz = differ_z(speed, 1, z, True) + differ(vz, hy[2], 0, True)
                rate = courant * shear[z]
                bulk = (courant * lame[z]) * (strain_x + strain_y + strain_z)
                twice = 2.0 * rate
                press = jnp.where(index[...] == z, edges[number, 2], 0.0)
                new = {
                    XX: stress_old[XX, z + 2] + (bulk + twice * strain_x),
                    YY: stress_old[YY, z + 2] + (bulk + twice * strain_y),
                    ZZ: stress_old[ZZ, z + 2] + (bulk + twice * strain_z) - press,
                    XY: stress_old[XY, z + 2] + rate * shear_xy,
                    XZ: stress_old[XZ, z + 2] + rate * shear_xz,
                    YZ: stress_old[YZ, z + 2] + rate * shear_yz,
                }
                write(new, z)
                if send:
                    for place, field in enumerate((XX, XY, XZ)):
                        parts[place] = packed(parts[place], new[field], inner)
            if send:
                begin(lambda d: rows_copy(number + 1, stress_b, d, chunk), has_y)
                return tuple(settle(h, p, chunk) for h, p in zip(held, parts))
            out_copy(chunk).start()
            return held

        return lax.fori_loop(0, chunks, body, zero_pack())

    def out_copy(chunk):
        layer = pl.ds(chunk * CHUNK, CHUNK)
        return pltpu.make_async_copy(
            stress_c.at[:, layer], wave_out.at[pl.ds(3, 6), layer], out_sem.at[chunk]
        )

    def centred(tile_o, halo, axis):
        return 0.5 * (shifted(tile_o, halo, axis, -1) - shifted(tile_o, halo, axis, 1))

    def around(tile_o, rows, cols):
        return (
            shifted(tile_o, cols, 1, -1)
            + shifted(tile_o, cols, 1, 1)
            + shifted(tile_o, rows, 0, -1)
            + shifted(tile_o, rows, 0, 1)
            - 4.0 * tile_o
        )

    def level_stage(number, speed, level, flux_x, flux_y):
        arrive(functools.partial(ocean_copy, number), has_y)
        side = columns(number, 3)
        rows_y = halo_o[number, 1]
        seafloor = none
        for z in range(layers // 2):
            seafloor = seafloor + jnp.where(index[...] == z, speed[2, z + 2], 0.0)
        spread = centred(flux_x, unpacked(side, 0), 1) + centred(flux_y, rows_y, 0)
        wet = wet_i[...].astype(jnp.float32)
        level = level + wet * (uplift * seafloor - ocean_rate * spread)
        edges[number + 1, 0] = level
        edges[number + 1, 2] = loading * (wet * level)
        begin(functools.partial(ocean_copy, number + 1), has_y)
        return level

    def flux_stage(number, level, flux_x, flux_y):
        arrive(functools.partial(ocean_copy, number + 1), has_y)
        side = columns(number, 3)
        level_side = unpacked(columns(number + 1, 3), 0)
        slope_x = centred(level, level_side, 1)
        slope_y = centred(level, halo_o[number + 1, 0], 0)
        wet = wet_i[...].astype(jnp.float32)
        around_x = around(flux_x, halo_o[number, 0], unpacked(side, 0))
        around_y = around(flux_y, halo_o[number, 1], unpacked(side, 1))
        pull = ocean_rate * depth[...]
        return (
            wet * (flux_x - pull * slope_x + viscous * around_x),
            wet * (flux_y - pull * slope_y + viscous * around_y),
        )

    def write_middle(new, z):
        for field, value in new.items():
            stress_b[field, z + 2] = value

    def write_last(new, z):
        for field, value in new.items():
            stress_c[STRESS_SOURCE[field] - 3, z] = value

    for copy in loads[:7]:
        copy.wait()
    level, flux_x, flux_y = ocean[0], ocean[1], ocean[2]
    held = lax.fori_loop(
        0, chunks, lambda chunk, held: pack_stress(stress_a, chunk, held), zero_pack()
    )
    finish_pack(0, held, (flux_x, flux_y))
    edges[0, 0] = flux_x
    edges[0, 1] = flux_y
    peers = sum(has.astype(jnp.int32) for has in (*has_y, *has_x))
    pl.semaphore_wait(barrier, peers)

    for chunk in range(chunks):
        begin(lambda d: rows_copy(0, stress_a, d, chunk), has_y)
    begin(functools.partial(columns_copy, 0), has_x)
    begin(functools.partial(ocean_copy, 0), has_y)
    for copy in loads[7:]:
        copy.wait()

    speeds = (speed_a, speed_b, speed_c)
    stresses = (stress_a, stress_b)
    for step in range(STEPS):
        number = 2 * step
        last = step == STEPS - 1
        held = velocity_stage(number, stresses[step], speeds[step], speeds[step + 1])
        new_level = level_stage(number, speeds[step + 1], level, flux_x, flux_y)
        finish_pack(number + 1, held, (new_level,))
        begin(functools.partial(columns_copy, number + 1), has_x)
        if last:
            speed_out = pltpu.make_async_copy(
                speed_c.at[:, pl.ds(2, layers)], wave_out.at[pl.ds(0, 3)], out_sem.at[chunks]
            )
            speed_out.start()
        held = stress_stage(
            number + 1,
            speeds[step + 1],
            stresses[step],
            write_last if last else write_middle,
            not last,
        )
        flux_x, flux_y = flux_stage(number, new_level, flux_x, flux_y)
        level = new_level
        if not last:
            edges[number + 2, 0] = flux_x
            edges[number + 2, 1] = flux_y
            finish_pack(number + 2, held, (flux_x, flux_y))
            begin(functools.partial(columns_copy, number + 2), has_x)
            begin(functools.partial(ocean_copy, number + 2), has_y)

    result_o[0] = level
    result_o[1] = flux_x
    result_o[2] = flux_y
    level_out = pltpu.make_async_copy(result_o, ocean_out, out_sem.at[chunks + 1])
    level_out.start()

    sources = (stress_a, speed_b, stress_b, speed_c)
    for number in range(2 * STEPS):

        def drain(chunk, carry):
            leave(lambda d: rows_copy(number, sources[number], d, chunk), has_y)
            return carry

        lax.fori_loop(0, chunks, drain, 0)
        leave(functools.partial(ocean_copy, number), has_y)
        leave(functools.partial(columns_copy, number), has_x)
    for chunk in range(chunks):
        out_copy(chunk).wait()
    speed_out.wait()
    level_out.wait()


def solution(mesh):
    counts = (mesh.shape["gx"], mesh.shape["gy"])

    def local(*arrays):
        fields, ocean = arrays[0], arrays[4]
        layers = fields.shape[1]
        chunks = layers // CHUNK
        f32, dma = jnp.float32, pltpu.SemaphoreType.DMA
        rounds = 2 * STEPS
        cube = (layers, 8, 128)
        padded = (layers + 4, 8, 128)
        return pl.pallas_call(
            functools.partial(kernel, counts),
            out_shape=(
                jax.ShapeDtypeStruct(fields.shape, f32),
                jax.ShapeDtypeStruct(ocean.shape, f32),
            ),
            in_specs=[pl.BlockSpec(memory_space=pl.ANY)] * 8,
            out_specs=(pl.BlockSpec(memory_space=pl.ANY), pl.BlockSpec(memory_space=pl.ANY)),
            scratch_shapes=[
                pltpu.VMEM((6, *padded), f32),
                pltpu.VMEM((3, *cube), f32),
                pltpu.VMEM(cube, f32),
                pltpu.VMEM(cube, f32),
                pltpu.VMEM(cube, f32),
                pltpu.VMEM((3, 8, 128), f32),
                pltpu.VMEM((8, 128), f32),
                pltpu.VMEM((8, 128), jnp.int32),
                pltpu.VMEM((8, 128), jnp.int32),
                pltpu.VMEM((6, *padded), f32),
                pltpu.VMEM((6, *cube), f32),
                pltpu.VMEM((3, *padded), f32),
                pltpu.VMEM((3, *padded), f32),
                pltpu.VMEM((rounds, 3, *cube), f32),
                pltpu.VMEM((rounds, 2, 8, 128), f32),
                pltpu.VMEM((rounds, 4, 8, 128), f32),
                pltpu.VMEM((rounds, 2, 4, 8, 128), f32),
                pltpu.VMEM((rounds, 3, 8, 128), f32),
                pltpu.VMEM((3, 8, 128), f32),
                dma((14,)),
                dma((chunks + 2,)),
                dma((rounds, 2, chunks)),
                dma((rounds, 2, chunks)),
                dma((rounds, 2)),
                dma((rounds, 2)),
                dma((rounds, 2)),
                dma((rounds, 2)),
            ],
            compiler_params=pltpu.CompilerParams(collective_id=0, has_side_effects=True),
            name="waves",
        )(*arrays)

    flat = P("gy", "gx")
    deep = P(None, "gy", "gx")
    in_specs = (P(None, None, "gy", "gx"), deep, deep, deep, deep, flat, flat, flat)
    out_specs = (P(None, None, "gy", "gx"), deep)
    return jax.shard_map(local, mesh=mesh, in_specs=in_specs, out_specs=out_specs, check_vma=False)
```

time: 323 us -> 33.5 us (0.10)
  the two profiles are of different devices: /device:TPU:18 before, /device:TPU:27 now
where the time goes in v1:
time: 33.5 us; the launch traced here: 33.1 us
  Pallas kernels  29.5 us (88%)
  local copies, waits for them, and re-layouts  2.97 us (9%)
  between operations  0.65 us (2%)
    pallas_call x1, Pallas kernels, local(): pl.pallas_call(functools.partial(kernel, counts), out_shape=(jax.ShapeDty...  29.5 us
    unnamed x4, local copies, waits for them, and re-layouts  2.97 us

profile of v1, /device:TPU:27, one launch (start us, length us, event | category | flops | bytes accessed | tf_op | source)
XLA Modules:
  0.0 33.1 jit_solution(18093464733081076476)
XLA Ops:
  0.6 29.5 %waves.1 = (f32[9,32,8,128]{3,2,1,0:T(8,128)}, f32[3,8,128]{2,1,0:T(8,128)}) custom-call(f32[9,32,8,128]{3,2,1,0:T(8,128)} %fields_ref.1, f32[32,8,128]{2,1,0:T(8,128)} %lame_ref.1, f32[32,8,128]{2,1,0:T(8,128)} %shear_ref.1, f32[32,8,128]{2,1,0:T(8,128)} %buoy_ref.1, f32[3,8,128]{2,1,0:T(8,128)} %ocean_ref.1, f32[8,128]{1,0:T(8,128)} %depth_ref.1, ...), custom_call_target="tpu_custom_call" | custom-call | tf_op jit(solution)/shard_map/waves/pallas_call | solution.py:465
  30.1 0.0 copy-start
  30.2 2.4 %copy.12 = f32[9,32,8,128]{3,2,1,0:T(8,128)} copy(f32[9,32,8,128]{3,2,1,0:T(8,128)} %get-tuple-element.4) | data formatting | bytes 2359296
  32.5 0.0 copy-done
  32.5 0.6 %copy.13 = f32[3,8,128]{2,1,0:T(8,128)} copy(f32[3,8,128]{2,1,0:T(8,128)S(1)} %copy-done) | data formatting | bytes 24576
Async XLA Ops:
  30.1 2.4 %copy-start = (f32[3,8,128]{2,1,0:T(8,128)S(1)}, f32[3,8,128]{2,1,0:T(8,128)}, u32[]{:S(2)}) copy-start(f32[3,8,128]{2,1,0:T(8,128)} %get-tuple-element.5) | copy-start | bytes 36868

commit v2 on v1

--- a/solution.py
+++ b/solution.py
@@ -48,7 +48,6 @@
     index,
     wet_i,
     stress_b,
-    stress_c,
     speed_b,
     speed_c,
     halo_y,
@@ -56,9 +55,7 @@
     pack,
     halo_x,
     edges,
-    result_o,
     load_sem,
-    out_sem,
     send_y,
     recv_y,
     send_o,
@@ -77,6 +74,14 @@
     to_y = ({"gy": jnp.minimum(at_y + 1, count_y - 1)}, {"gy": jnp.maximum(at_y - 1, 0)})
     to_x = ({"gx": jnp.minimum(at_x + 1, count_x - 1)}, {"gx": jnp.maximum(at_x - 1, 0)})
 
+    barrier = pltpu.get_barrier_semaphore()
+    for has, to in ((has_y, to_y), (has_x, to_x)):
+        for direction in range(2):
+
+            @pl.when(has[direction])
+            def _():
+                pl.semaphore_signal(barrier, inc=1, device_id=to[direction])
+
     loads = []
 
     def load(source, target):
@@ -118,14 +123,6 @@
             for number in range(2 * STEPS):
                 for place in range(4):
                     halo_x[number, direction, place] = none
-
-    barrier = pltpu.get_barrier_semaphore()
-    for has, to in ((has_y, to_y), (has_x, to_x)):
-        for direction in range(2):
-
-            @pl.when(has[direction])
-            def _():
-                pl.semaphore_signal(barrier, inc=1, device_id=to[direction])
 
     for stress in (stress_a, stress_b):
         for field in (YZ, XZ, ZZ):
@@ -276,6 +273,8 @@
                     old = speed_old[field, z] if speed_old is speed_a else speed_old[field, z + 2]
                     new = old + rate * push
                     speed_new[field, z + 2] = new
+                    if speed_new is speed_c:
+                        wave_out[field, z] = new
                     parts[field] = packed(parts[field], new, inner)
             begin(lambda d: rows_copy(number + 1, speed_new, d, chunk), has_y)
             return tuple(settle(h, p, chunk) for h, p in zip(held, parts))
@@ -319,16 +318,9 @@
             if send:
                 begin(lambda d: rows_copy(number + 1, stress_b, d, chunk), has_y)
                 return tuple(settle(h, p, chunk) for h, p in zip(held, parts))
-            out_copy(chunk).start()
             return held
 
         return lax.fori_loop(0, chunks, body, zero_pack())
-
-    def out_copy(chunk):
-        layer = pl.ds(chunk * CHUNK, CHUNK)
-        return pltpu.make_async_copy(
-            stress_c.at[:, layer], wave_out.at[pl.ds(3, 6), layer], out_sem.at[chunk]
-        )
 
     def centred(tile_o, halo, axis):
         return 0.5 * (shifted(tile_o, halo, axis, -1) - shifted(tile_o, halo, axis, 1))
@@ -378,7 +370,7 @@
 
     def write_last(new, z):
         for field, value in new.items():
-            stress_c[STRESS_SOURCE[field] - 3, z] = value
+            wave_out[STRESS_SOURCE[field], z] = value
 
     for copy in loads[:7]:
         copy.wait()
@@ -408,11 +400,6 @@
         new_level = level_stage(number, speeds[step + 1], level, flux_x, flux_y)
         finish_pack(number + 1, held, (new_level,))
         begin(functools.partial(columns_copy, number + 1), has_x)
-        if last:
-            speed_out = pltpu.make_async_copy(
-                speed_c.at[:, pl.ds(2, layers)], wave_out.at[pl.ds(0, 3)], out_sem.at[chunks]
-            )
-            speed_out.start()
         held = stress_stage(
             number + 1,
             speeds[step + 1],
@@ -429,11 +416,9 @@
             begin(functools.partial(columns_copy, number + 2), has_x)
             begin(functools.partial(ocean_copy, number + 2), has_y)
 
-    result_o[0] = level
-    result_o[1] = flux_x
-    result_o[2] = flux_y
-    level_out = pltpu.make_async_copy(result_o, ocean_out, out_sem.at[chunks + 1])
-    level_out.start()
+    ocean_out[0] = level
+    ocean_out[1] = flux_x
+    ocean_out[2] = flux_y
 
     sources = (stress_a, speed_b, stress_b, speed_c)
     for number in range(2 * STEPS):
@@ -445,10 +430,17 @@
         lax.fori_loop(0, chunks, drain, 0)
         leave(functools.partial(ocean_copy, number), has_y)
         leave(functools.partial(columns_copy, number), has_x)
-    for chunk in range(chunks):
-        out_copy(chunk).wait()
-    speed_out.wait()
-    level_out.wait()
+
+
+def hand_on(waves, sea, waves_out, sea_out, sem):
+    copies = [
+        pltpu.make_async_copy(waves, waves_out, sem.at[0]),
+        pltpu.make_async_copy(sea, sea_out, sem.at[1]),
+    ]
+    for copy in copies:
+        copy.start()
+    for copy in copies:
+        copy.wait()
 
 
 def solution(mesh):
@@ -462,14 +454,14 @@
         rounds = 2 * STEPS
         cube = (layers, 8, 128)
         padded = (layers + 4, 8, 128)
-        return pl.pallas_call(
+        waves, sea = pl.pallas_call(
             functools.partial(kernel, counts),
             out_shape=(
-                jax.ShapeDtypeStruct(fields.shape, f32),
-                jax.ShapeDtypeStruct(ocean.shape, f32),
+                pltpu.VMEM(fields.shape, f32),
+                pltpu.VMEM(ocean.shape, f32),
             ),
             in_specs=[pl.BlockSpec(memory_space=pl.ANY)] * 8,
-            out_specs=(pl.BlockSpec(memory_space=pl.ANY), pl.BlockSpec(memory_space=pl.ANY)),
+            out_specs=(pl.BlockSpec(memory_space=pltpu.VMEM), pl.BlockSpec(memory_space=pltpu.VMEM)),
             scratch_shapes=[
                 pltpu.VMEM((6, *padded), f32),
                 pltpu.VMEM((3, *cube), f32),
@@ -481,7 +473,6 @@
                 pltpu.VMEM((8, 128), jnp.int32),
                 pltpu.VMEM((8, 128), jnp.int32),
                 pltpu.VMEM((6, *padded), f32),
-                pltpu.VMEM((6, *cube), f32),
                 pltpu.VMEM((3, *padded), f32),
                 pltpu.VMEM((3, *padded), f32),
                 pltpu.VMEM((rounds, 3, *cube), f32),
@@ -489,9 +480,7 @@
                 pltpu.VMEM((rounds, 4, 8, 128), f32),
                 pltpu.VMEM((rounds, 2, 4, 8, 128), f32),
                 pltpu.VMEM((rounds, 3, 8, 128), f32),
-                pltpu.VMEM((3, 8, 128), f32),
                 dma((14,)),
-                dma((chunks + 2,)),
                 dma((rounds, 2, chunks)),
                 dma((rounds, 2, chunks)),
                 dma((rounds, 2)),
@@ -499,9 +488,21 @@
                 dma((rounds, 2)),
                 dma((rounds, 2)),
             ],
-            compiler_params=pltpu.CompilerParams(collective_id=0, has_side_effects=True),
+            compiler_params=pltpu.CompilerParams(collective_id=0, has_side_effects=True, vmem_limit_bytes=60 << 20),
             name="waves",
         )(*arrays)
+        return pl.pallas_call(
+            hand_on,
+            out_shape=(
+                jax.ShapeDtypeStruct(fields.shape, f32),
+                jax.ShapeDtypeStruct(ocean.shape, f32),
+            ),
+            in_specs=[pl.BlockSpec(memory_space=pltpu.VMEM)] * 2,
+            out_specs=(pl.BlockSpec(memory_space=pl.ANY), pl.BlockSpec(memory_space=pl.ANY)),
+            scratch_shapes=[dma((2,))],
+            compiler_params=pltpu.CompilerParams(vmem_limit_bytes=12 << 20),
+            name="hand_on",
+        )(waves, sea)
 
     flat = P("gy", "gx")
     deep = P(None, "gy", "gx")

time: 33.5 us -> 30.9 us (0.922)
  local copies, waits for them, and re-layouts: 2.97 us -> 0 us
  Pallas kernels: 29.5 us -> 30 us
    unnamed x4 -> x0, local copies, waits for them, and re-layouts: 2.97 us -> none
    pallas_call x1 -> x2, Pallas kernels: 29.5 us -> 30 us  [the longest x1 29 us: local(): pl.pallas_call(functools.partial(kernel, counts), out_shape=(pltpu.VMEM(f...]
where the time goes in v2:
time: 30.9 us; the launch traced here: 30.6 us
  Pallas kernels  30 us (97%)
  between operations  0.64 us (2%)
    pallas_call x1, Pallas kernels, local(): pl.pallas_call(functools.partial(kernel, counts), out_shape=(pltpu.VMEM(f...  29 us
    pallas_call x1, Pallas kernels, local(): pl.pallas_call(hand_on, out_shape=(jax.ShapeDtypeStruct(fields.shape, f32...  1.03 us

profile of v2, /device:TPU:27, one launch (start us, length us, event | category | flops | bytes accessed | tf_op | source)
XLA Modules:
  0.0 30.6 jit_solution(11176523804696374720)
XLA Ops:
  0.6 29.0 %waves.1 = (f32[9,32,8,128]{3,2,1,0:T(8,128)S(1)}, f32[3,8,128]{2,1,0:T(8,128)S(1)}) custom-call(f32[9,32,8,128]{3,2,1,0:T(8,128)} %fields_ref.1, f32[32,8,128]{2,1,0:T(8,128)} %lame_ref.1, f32[32,8,128]{2,1,0:T(8,128)} %shear_ref.1, f32[32,8,128]{2,1,0:T(8,128)} %buoy_ref.1, f32[3,8,128]{2,1,0:T(8,128)} %ocean_ref.1, f32[8,128]{1,0:T(8,128)} %depth_ref.1, ...), custom_call_target="tpu_custom_call" | custom-call | tf_op jit(solution)/shard_map/waves/pallas_call | solution.py:457
  29.6 1.0 %hand_on.1 = (f32[9,32,8,128]{3,2,1,0:T(8,128)}, f32[3,8,128]{2,1,0:T(8,128)}) custom-call(f32[9,32,8,128]{3,2,1,0:T(8,128)S(1)} %get-tuple-element.4.waves, f32[3,8,128]{2,1,0:T(8,128)S(1)} %get-tuple-element.5.sea), custom_call_target="tpu_custom_call" | custom-call | tf_op jit(solution)/shard_map/hand_on/pallas_call | solution.py:494

commit v3 on v0

v3 whole, which is shorter than its diff:
```python
import functools

import jax
import jax.numpy as jnp
from jax import lax
from jax.experimental import pallas as pl
from jax.experimental.pallas import tpu as pltpu
from jax.sharding import PartitionSpec as P

STEPS = 2
CHUNK = 8
TILE = (8, 128)

near = 9.0 / 8.0
far = -1.0 / 24.0
courant = 0.3
ocean_rate = 0.3
uplift = 0.5
loading = 0.5
viscous = 0.1

XX, YY, ZZ, XY, XZ, YZ = range(6)
ALONG_X = ((XX, True), (XY, False), (XZ, False))
ALONG_Y = ((XY, False), (YY, True), (YZ, False))
FIELD = (0, 2, 1)
ALONG_Z = ((XZ, False), (YZ, False), (ZZ, True))


def turned(tile, shift, axis):
    return pltpu.roll(tile, shift % tile.shape[axis], axis)


def kernel(
    counts,
    fields_ref,
    lame_ref,
    shear_ref,
    buoy_ref,
    ocean_ref,
    depth_ref,
    index_ref,
    wet_ref,
    wave_out,
    ocean_out,
    stress_a,
    stress_b,
    speed_a,
    speed_b,
    speed_c,
    lame,
    shear,
    buoy,
    sea,
    depth,
    index,
    wet_i,
    press,
    pushed,
    wraps,
    packs,
    rows_o,
    packs_o,
    halo_wraps,
    halo_pushed,
    halo_buoy,
    halo_x,
    halo_d,
    halo_oy,
    halo_ox,
    halo_od,
    speed_rows,
    speed_cols,
    load_sem,
    send_y,
    recv_y,
    send_b,
    recv_b,
    send_x,
    recv_x,
    send_d,
    recv_d,
    send_oy,
    recv_oy,
    send_ox,
    recv_ox,
    send_od,
    recv_od,
):
    count_x, count_y = counts
    at_x, at_y = lax.axis_index("gx"), lax.axis_index("gy")
    layers = fields_ref.shape[1]
    chunks = layers // CHUNK

    next_x = (jnp.minimum(at_x + 1, count_x - 1), jnp.maximum(at_x - 1, 0))
    next_y = (jnp.minimum(at_y + 1, count_y - 1), jnp.maximum(at_y - 1, 0))
    inside_x = (at_x < count_x - 1, at_x > 0)
    inside_y = (at_y < count_y - 1, at_y > 0)
    to_y = tuple({"gy": y} for y in next_y)
    to_x = tuple({"gx": x} for x in next_x)
    to_d = tuple({"gx": next_x[d // 2], "gy": next_y[d % 2]} for d in range(4))
    inside_d = tuple(jnp.logical_and(inside_x[d // 2], inside_y[d % 2]) for d in range(4))

    def each(inside, act):
        for direction, there in enumerate(inside):
            pl.when(there)(functools.partial(act, direction))

    from_x = inside_x[::-1]
    from_y = inside_y[::-1]
    from_d = inside_d[::-1]

    barrier = pltpu.get_barrier_semaphore()
    for inside, to in ((inside_y, to_y), (inside_d, to_d), (inside_x, to_x)):
        each(
            inside,
            lambda d, to=to: pl.semaphore_signal(barrier, inc=1, device_id=to[d]),
        )

    loads = []

    def load(source, target):
        copy = pltpu.make_async_copy(source, target, load_sem.at[len(loads)])
        copy.start()
        loads.append(copy)

    inner_layers = pl.ds(2, layers)
    load(fields_ref.at[pl.ds(3, 6)], stress_a.at[:, inner_layers])
    load(fields_ref.at[pl.ds(0, 3)], speed_a.at[:, inner_layers])
    load(buoy_ref, buoy.at[pl.ds(0, layers)])
    load(ocean_ref, sea.at[0])
    load(depth_ref, depth)
    load(index_ref, index)
    load(wet_ref, wet_i)
    load(lame_ref, lame)
    load(shear_ref, shear)

    none = jnp.zeros(TILE, jnp.float32)
    row_at = lax.broadcasted_iota(jnp.int32, TILE, 0)
    lane_at = lax.broadcasted_iota(jnp.int32, TILE, 1)
    group_at = lane_at // 4
    slot_at = lane_at % 4
    low_slot = slot_at < 2
    upper = row_at < 4
    edge_rows = jnp.logical_or(row_at < 2, row_at >= 6)
    edge_lanes = jnp.logical_or(lane_at < 2, lane_at >= 126)
    wrap_back = jnp.logical_or(row_at < 2, row_at >= 7)
    wrap_ahead = jnp.logical_or(row_at < 1, row_at >= 6)
    wrap_rows = (wrap_back, wrap_ahead, wrap_back)

    margins = (0, 1, layers + 2, layers + 3)
    for z in margins:
        for field in (XZ, YZ, ZZ):
            stress_a[field, z] = none
            stress_b[field, z] = none
        for field in range(3):
            speed_b[field, z] = none
            speed_c[field, z] = none

    wrap_parts = ((pl.ds(0, 2), (pl.ds(0, 2), pl.ds(7, 1))), (pl.ds(2, 1), (pl.ds(0, 1), pl.ds(6, 2))))
    push_parts = ((pl.ds(0, 2), (pl.ds(7, 1), pl.ds(0, 2))), (pl.ds(2, 1), (pl.ds(6, 2), pl.ds(0, 1))))

    def layers_of(chunk):
        return pl.ds(0, layers) if chunk is None else pl.ds(chunk * CHUNK, CHUNK)

    def rows_copies(step, direction, chunk, which):
        source, target = ((wraps, halo_wraps), (pushed, halo_pushed))[which]
        result = []
        for part, (fields, rows) in enumerate((wrap_parts, push_parts)[which]):
            box = (step, fields, layers_of(chunk), rows[direction], slice(None))
            result.append(
                pltpu.make_async_remote_copy(
                    source.at[box],
                    target.at[box],
                    send_y.at[step, direction, which, part],
                    recv_y.at[step, direction, which, part, 0 if chunk is None else chunk],
                    device_id=to_y[direction],
                )
            )
        return result

    def buoy_copy(direction):
        rows = pl.ds(6, 2) if direction == 0 else pl.ds(0, 2)
        return pltpu.make_async_remote_copy(
            buoy_ref.at[:, rows, :],
            halo_buoy.at[:, rows, :],
            send_b.at[direction],
            recv_b.at[direction],
            device_id=to_y[direction],
        )

    def chunk_at(chunk):
        return pl.ds(0, chunks) if chunk is None else pl.ds(chunk, 1)

    def columns_copy(step, direction, chunk):
        return pltpu.make_async_remote_copy(
            packs.at[step, chunk_at(chunk), pl.ds(0, 2)],
            halo_x.at[step, direction, chunk_at(chunk)],
            send_x.at[step, direction],
            recv_x.at[step, direction, 0 if chunk is None else chunk],
            device_id=to_x[direction],
        )

    def corner_copy(step, corner, chunk):
        rows = pl.ds(4, 4) if corner % 2 == 0 else pl.ds(0, 4)
        return pltpu.make_async_remote_copy(
            packs.at[step, chunk_at(chunk), 2, rows, :],
            halo_d.at[step, corner, chunk_at(chunk), rows, :],
            send_d.at[step, corner],
            recv_d.at[step, corner, 0 if chunk is None else chunk],
            device_id=to_d[corner],
        )

    def ocean_rows(step, direction):
        row = pl.ds(7, 1) if direction == 0 else pl.ds(0, 1)
        return pltpu.make_async_remote_copy(
            rows_o.at[step, :, row, :],
            halo_oy.at[step, :, row, :],
            send_oy.at[step, direction],
            recv_oy.at[step, direction],
            device_id=to_y[direction],
        )

    def ocean_columns(step, direction):
        return pltpu.make_async_remote_copy(
            packs_o.at[step],
            halo_ox.at[step, direction],
            send_ox.at[step, direction],
            recv_ox.at[step, direction],
            device_id=to_x[direction],
        )

    def ocean_corner(step, corner):
        return pltpu.make_async_remote_copy(
            packs_o.at[step],
            halo_od.at[step, corner],
            send_od.at[step, corner],
            recv_od.at[step, corner],
            device_id=to_d[corner],
        )

    def start_chunk(step, chunk):
        def start_rows(direction):
            for which in range(2):
                for copy in rows_copies(step, direction, chunk, which):
                    copy.start()

        each(inside_y, start_rows)
        each(inside_d, lambda d: corner_copy(step, d, chunk).start())
        each(inside_x, lambda d: columns_copy(step, d, chunk).start())

    def start_ocean(step):
        each(inside_y, lambda d: ocean_rows(step, d).start())
        each(inside_d, lambda d: ocean_corner(step, d).start())
        each(inside_x, lambda d: ocean_columns(step, d).start())

    def wait_rows(step, chunk, which):
        def wait(direction):
            for copy in rows_copies(step, direction, chunk, which):
                copy.wait_recv()

        each(from_y, wait)

    def drain(step):
        def rows(direction):
            for which in range(2):
                for copy in rows_copies(step, direction, None, which):
                    copy.wait_send()
            ocean_rows(step, direction).wait_send()
            if step == 0:
                buoy_copy(direction).wait_send()

        def corner(d):
            corner_copy(step, d, None).wait_send()
            ocean_corner(step, d).wait_send()

        def columns(direction):
            columns_copy(step, direction, None).wait_send()
            ocean_columns(step, direction).wait_send()

        each(inside_y, rows)
        each(inside_d, corner)
        each(inside_x, columns)

    def clear_rows(direction):
        first = direction == 0
        push_rows = slice(6, 8) if first else slice(0, 2)
        wrap_rows = slice(0, 2) if first else slice(6, 8)
        zeros = jnp.zeros((2, 128), jnp.float32)

        def clear(z, carry):
            halo_buoy[z, push_rows, :] = zeros
            for step in range(STEPS):
                for field in range(3):
                    halo_pushed[step, field, z, push_rows, :] = zeros
                    halo_wraps[step, field, z, wrap_rows, :] = zeros
            return carry

        lax.fori_loop(0, layers, clear, 0)
        for step in range(STEPS):
            for item in range(5):
                halo_oy[step, item, push_rows, :] = zeros

    def clear_columns(direction):
        for step in range(STEPS):
            halo_ox[step, direction] = none
            for chunk in range(chunks):
                for part in range(2):
                    halo_x[step, direction, chunk, part] = none

    def clear_corner(corner):
        for step in range(STEPS):
            halo_od[step, corner] = none
            for chunk in range(chunks):
                halo_d[step, corner, chunk] = none

    each(tuple(jnp.logical_not(there) for there in from_y), clear_rows)
    each(tuple(jnp.logical_not(there) for there in from_x), clear_columns)
    each(tuple(jnp.logical_not(there) for there in from_d), clear_corner)

    def packed(held, tile, place):
        return jnp.where(group_at == place, turned(tile, 2 + 4 * place, 1), held)

    def unpacked(part, place):
        return turned(part, -(2 + 4 * place), 1)

    def shifted(tile, halo, axis, by):
        at, size = (row_at, 8) if axis == 0 else (lane_at, 128)
        from_halo = at >= size - by if by > 0 else at < -by
        return turned(jnp.where(from_halo, halo, tile), by, axis)

    def differ(tile, halo, axis, forward):
        before = shifted(tile, halo, axis, 1)
        after = shifted(tile, halo, axis, -1)
        if forward:
            after_two = shifted(tile, halo, axis, -2)
            return near * (after - tile) + far * (after_two - before)
        before_two = shifted(tile, halo, axis, 2)
        return near * (tile - before) + far * (after - before_two)

    def differ_z(ref, field, z, forward):
        at = [ref[field, z + 2 + k] for k in ((-1, 0, 1, 2) if forward else (-2, -1, 0, 1))]
        return near * (at[2] - at[1]) + far * (at[3] - at[0])

    def weight(mask, value):
        return jnp.where(mask, jnp.float32(value), jnp.float32(0.0))

    def wrapped(tile, axis, forward, low_one, low_two, high_one, high_two):
        before, after = turned(tile, 1, axis), turned(tile, -1, axis)
        if forward:
            return (
                weight(low_one, -far) * before
                + weight(high_one, near) * after
                + weight(high_two, far) * turned(tile, -2, axis)
            )
        return (
            weight(low_one, -near) * before
            + weight(low_two, -far) * turned(tile, 2, axis)
            + weight(high_one, far) * after
        )

    row_ends = (row_at < 1, row_at < 2, row_at >= 7, row_at >= 6)
    slot_ends = (slot_at == 2, slot_at >= 2, slot_at == 1, slot_at < 2)

    def circular_y(tile, forward):
        before, after = turned(tile, 1, 0), turned(tile, -1, 0)
        low_one, low_two, high_one, high_two = row_ends
        if forward:
            two = turned(tile, -2, 0)
            whole = near * (after - tile) + far * (two - before)
            wrap = (
                weight(low_one, -far) * before
                + weight(high_one, near) * after
                + weight(high_two, far) * two
            )
        else:
            two = turned(tile, 2, 0)
            whole = near * (tile - before) + far * (after - two)
            wrap = (
                weight(low_one, -near) * before
                + weight(low_two, -far) * two
                + weight(high_one, far) * after
            )
        return whole - wrap, wrap

    def local_x(tile, forward):
        before, after = turned(tile, 1, 1), turned(tile, -1, 1)
        if forward:
            two = turned(tile, -2, 1)
            return (
                weight(lane_at < 127, near) * after
                - near * tile
                + weight(lane_at < 126, far) * two
                - weight(lane_at >= 1, far) * before
            )
        two = turned(tile, 2, 1)
        return (
            near * tile
            - weight(lane_at >= 1, near) * before
            + weight(lane_at < 127, far) * after
            - weight(lane_at >= 2, far) * two
        )

    def push_chunk(step, chunk, stress, speed):
        edge_push, edge_x, edge_y = none, none, none
        for inner in range(CHUNK):
            z = chunk * CHUNK + inner
            rate = courant * buoy[z]
            edge_push = packed(edge_push, rate, 3 * CHUNK + inner)
            for axis in range(3):
                tile_x, tile_y = stress[ALONG_X[axis][0], z + 2], stress[ALONG_Y[axis][0], z + 2]
                kept, wrap = circular_y(tile_y, ALONG_Y[axis][1])
                total = (
                    local_x(tile_x, ALONG_X[axis][1])
                    + kept
                    + differ_z(stress, ALONG_Z[axis][0], z, ALONG_Z[axis][1])
                )
                push = speed[axis, z + 2] + rate * total
                pushed[step, FIELD[axis], z] = push
                wraps[step, FIELD[axis], z] = wrap
                place = axis * CHUNK + inner
                edge_push = packed(edge_push, push, place)
                edge_x = packed(edge_x, tile_x, place)
                edge_y = packed(edge_y, tile_y, place)
        first = lane_at < 4 * CHUNK
        second = jnp.logical_and(lane_at >= 4 * CHUNK, lane_at < 8 * CHUNK)
        packs[step, chunk, 0] = edge_push
        wrap_x = jnp.where(
            first, wrapped(edge_x, 1, True, *slot_ends), wrapped(edge_x, 1, False, *slot_ends)
        )
        packs[step, chunk, 1] = wrap_x
        wrap_y = jnp.where(
            second, wrapped(edge_y, 0, True, *row_ends), wrapped(edge_y, 0, False, *row_ends)
        )
        packs[step, chunk, 2] = jnp.where(edge_rows, wrap_x, turned(wrap_y, 4, 0))

    def join_chunk(step, chunk, speed):
        side = jnp.where(low_slot, halo_x[step, 1, chunk, 1], halo_x[step, 0, chunk, 1])
        for inner in range(CHUNK):
            z = chunk * CHUNK + inner
            rate = courant * buoy[z]
            for axis in range(3):
                added = jnp.where(wrap_rows[axis], halo_wraps[step, FIELD[axis], z], 0.0) + jnp.where(
                    edge_lanes, unpacked(side, axis * CHUNK + inner), 0.0
                )
                new = pushed[step, FIELD[axis], z] + rate * added
                speed[axis, z + 2] = new
                if step == STEPS - 1:
                    wave_out[axis, z] = new

    def corners(step, chunk):
        def of(dx):
            return jnp.where(
                upper, halo_d[step, 2 * dx + 1, chunk], halo_d[step, 2 * dx, chunk]
            )

        low, high = of(0), of(1)
        wrap_y = turned(jnp.where(low_slot, low, high), 4, 0)
        return jnp.where(low_slot, high, low), jnp.where(edge_rows, wrap_y, 0.0)

    def halo_chunk(step, chunk):
        wrap_x, wrap_y = corners(step, chunk)
        edge = jnp.where(low_slot, halo_x[step, 0, chunk, 0], halo_x[step, 1, chunk, 0])
        span = lane_at // (4 * CHUNK)
        rate_edge = jnp.where(
            span == 0,
            turned(edge, 4 * CHUNK, 1),
            jnp.where(span == 1, turned(edge, 8 * CHUNK, 1), turned(edge, 12 * CHUNK, 1)),
        )
        speed_cols[step, chunk] = edge + rate_edge * (packs[step, chunk, 1] + wrap_y)
        for inner in range(CHUNK):
            z = chunk * CHUNK + inner
            rate = courant * halo_buoy[z]
            for axis in range(3):
                added = wraps[step, FIELD[axis], z] + jnp.where(
                    edge_lanes, unpacked(wrap_x, axis * CHUNK + inner), 0.0
                )
                speed_rows[axis, z] = halo_pushed[step, FIELD[axis], z] + rate * added

    def stress_chunk(step, chunk, speed, stress_old, stress_new):
        side = speed_cols[step, chunk]
        for inner in range(CHUNK):
            z = chunk * CHUNK + inner
            vx, vy, vz = speed[0, z + 2], speed[1, z + 2], speed[2, z + 2]
            hx = [unpacked(side, axis * CHUNK + inner) for axis in range(3)]
            hy = [speed_rows[axis, z] for axis in range(3)]
            strain_x = differ(vx, hx[0], 1, False)
            strain_y = differ(vy, hy[1], 0, False)
            strain_z = differ_z(speed, 2, z, False)
            shear_xy = differ(vx, hy[0], 0, True) + differ(vy, hx[1], 1, True)
            shear_xz = differ_z(speed, 0, z, True) + differ(vz, hx[2], 1, True)
            shear_yz = differ_z(speed, 1, z, True) + differ(vz, hy[2], 0, True)
            rate = courant * shear[z]
            bulk = (courant * lame[z]) * (strain_x + strain_y + strain_z)
            twice = 2.0 * rate
            load_z = jnp.where(index[...] == z, press[step], 0.0)
            new = {
                XX: stress_old[XX, z + 2] + (bulk + twice * strain_x),
                YY: stress_old[YY, z + 2] + (bulk + twice * strain_y),
                ZZ: stress_old[ZZ, z + 2] + (bulk + twice * strain_z) - load_z,
                XY: stress_old[XY, z + 2] + rate * shear_xy,
                XZ: stress_old[XZ, z + 2] + rate * shear_xz,
                YZ: stress_old[YZ, z + 2] + rate * shear_yz,
            }
            for field, value in new.items():
                if step == STEPS - 1:
                    wave_out[3 + field, z] = value
                else:
                    stress_new[field, z + 2] = value

    def centred(tile, halo, axis):
        return 0.5 * (shifted(tile, halo, axis, -1) - shifted(tile, halo, axis, 1))

    def around(tile, rows, cols):
        return (
            shifted(tile, cols, 1, -1)
            + shifted(tile, cols, 1, 1)
            + shifted(tile, rows, 0, -1)
            + shifted(tile, rows, 0, 1)
            - 4.0 * tile
        )

    def ocean_prepare(step):
        level, flux_x, flux_y = sea[step, 0], sea[step, 1], sea[step, 2]
        wet = wet_i[...].astype(jnp.float32)
        spread = centred(flux_x, none, 1) + centred(flux_y, none, 0)
        items = (
            flux_x,
            flux_y,
            level - ocean_rate * (wet * spread),
            wet,
            index[...].astype(jnp.float32),
        )
        pack = none
        for place, item in enumerate(items):
            rows_o[step, place] = item
            pack = packed(pack, item, place)
        packs_o[step] = pack

    def ocean_edge(step):
        return jnp.where(low_slot, halo_ox[step, 0], halo_ox[step, 1])

    def ocean_level(step, speed):
        level, flux_x, flux_y = sea[step, 0], sea[step, 1], sea[step, 2]
        wet = wet_i[...].astype(jnp.float32)
        seafloor = none
        for z in range(layers // 2):
            seafloor = seafloor + jnp.where(index[...] == z, speed[2, z + 2], 0.0)
        spread = centred(flux_x, unpacked(ocean_edge(step), 0), 1) + centred(
            flux_y, halo_oy[step, 1], 0
        )
        level = level + wet * (uplift * seafloor - ocean_rate * spread)
        sea[step + 1, 0] = level
        press[step] = loading * (wet * level)

    def ocean_flux(step):
        level, flux_x, flux_y = sea[step + 1, 0], sea[step, 1], sea[step, 2]
        wet = wet_i[...].astype(jnp.float32)
        edge = ocean_edge(step)

        def of(dx):
            return jnp.where(upper, halo_od[step, 2 * dx + 1], halo_od[step, 2 * dx])

        corner = jnp.where(low_slot, of(0), of(1))

        index_rows = halo_oy[step, 4]
        seafloor = none
        for z in range(layers // 2):
            seafloor = seafloor + jnp.where(index_rows == z, speed_rows[2, z], 0.0)
        spread = centred(none, flux_y, 0) + centred(none, unpacked(corner, 0), 1)
        level_rows = halo_oy[step, 2] + halo_oy[step, 3] * (
            uplift * seafloor - ocean_rate * spread
        )

        own = packs_o[step]
        index_edge = jnp.where(lane_at < 4, turned(edge, -16, 1), 0.0)
        for by in (4, 8, 16):
            index_edge = index_edge + turned(index_edge, by, 1)
        index_edge = turned(index_edge, 8 * CHUNK, 1)
        total = none
        for chunk in range(layers // 2 // CHUNK):
            z_at = chunk * CHUNK + group_at - 2 * CHUNK
            chosen = jnp.logical_and(
                index_edge == z_at.astype(jnp.float32), lane_at // (4 * CHUNK) == 2
            )
            total = total + jnp.where(chosen, speed_cols[step, chunk], 0.0)
        total = turned(total, -8 * CHUNK, 1)
        for by in (16, 8, 4):
            total = total + turned(total, -by, 1)
        spread_edge = (
            jnp.where(slot_at == 1, 0.5 * turned(own, -1, 1), 0.0)
            - jnp.where(slot_at == 2, 0.5 * turned(own, 1, 1), 0.0)
            + centred(none, turned(corner, -4, 1), 0)
        )
        level_edge = turned(edge, -8, 1) + turned(edge, -12, 1) * (
            uplift * total - ocean_rate * spread_edge
        )

        slope_x = centred(level, unpacked(level_edge, 0), 1)
        slope_y = centred(level, level_rows, 0)
        around_x = around(flux_x, halo_oy[step, 0], unpacked(edge, 0))
        around_y = around(flux_y, halo_oy[step, 1], unpacked(edge, 1))
        pull = ocean_rate * depth[...]
        sea[step + 1, 1] = wet * (flux_x - pull * slope_x + viscous * around_x)
        sea[step + 1, 2] = wet * (flux_y - pull * slope_y + viscous * around_y)

    for copy in loads[:7]:
        copy.wait()
    speeds = (speed_a, speed_b, speed_c)
    stresses = (stress_a, stress_b, stress_b)

    def first_push(chunk, carry):
        push_chunk(0, chunk, stress_a, speed_a)
        return carry

    lax.fori_loop(0, chunks, first_push, 0)
    ocean_prepare(0)

    peers = sum(there.astype(jnp.int32) for there in (*inside_x, *inside_y, *inside_d))
    pl.semaphore_wait(barrier, peers)

    def first_send(chunk, carry):
        start_chunk(0, chunk)
        return carry

    start_chunk(0, 0)
    each(inside_y, lambda d: buoy_copy(d).start())
    start_ocean(0)
    lax.fori_loop(1, chunks, first_send, 0)
    for copy in loads[7:]:
        copy.wait()

    for step in range(STEPS):
        last = step == STEPS - 1
        speed_old, speed_new = speeds[step], speeds[step + 1]
        stress_old, stress_new = stresses[step], stresses[step + 1]

        def body(turn, carry):
            @pl.when(turn < chunks)
            def _():
                each(from_x, lambda d: columns_copy(step, d, turn).wait_recv())
                wait_rows(step, turn, 0)
                join_chunk(step, turn, speed_new)

            @pl.when(turn == 1)
            def _():
                each(from_x, lambda d: ocean_columns(step, d).wait_recv())
                each(from_y, lambda d: ocean_rows(step, d).wait_recv())
                ocean_level(step, speed_new)
                if step == 0:
                    each(from_y, lambda d: buoy_copy(d).wait_recv())

            @pl.when(jnp.logical_and(turn >= 1, turn <= chunks))
            def _():
                wait_rows(step, turn - 1, 1)
                each(from_d, lambda d: corner_copy(step, d, turn - 1).wait_recv())
                halo_chunk(step, turn - 1)
                stress_chunk(step, turn - 1, speed_new, stress_old, stress_new)

            @pl.when(turn == 2)
            def _():
                each(from_d, lambda d: ocean_corner(step, d).wait_recv())
                ocean_flux(step)
                if not last:
                    ocean_prepare(step + 1)
                    start_ocean(step + 1)

            if not last:

                @pl.when(turn >= 2)
                def _():
                    push_chunk(step + 1, turn - 2, stress_new, speed_new)
                    start_chunk(step + 1, turn - 2)

            return carry

        lax.fori_loop(0, chunks + (1 if last else 2), body, 0)
        drain(step)

    for item in range(3):
        ocean_out[item] = sea[STEPS, item]


def hand_on(waves, sea, waves_out, sea_out, sem):
    copies = [
        pltpu.make_async_copy(waves, waves_out, sem.at[0]),
        pltpu.make_async_copy(sea, sea_out, sem.at[1]),
    ]
    for copy in copies:
        copy.start()
    for copy in copies:
        copy.wait()


def solution(mesh):
    counts = (mesh.shape["gx"], mesh.shape["gy"])

    def local(*arrays):
        fields, ocean = arrays[0], arrays[4]
        layers = fields.shape[1]
        chunks = layers // CHUNK
        f32, dma = jnp.float32, pltpu.SemaphoreType.DMA
        cube = (layers, *TILE)
        padded = (layers + 4, *TILE)
        waves, sea = pl.pallas_call(
            functools.partial(kernel, counts),
            out_shape=(pltpu.VMEM(fields.shape, f32), pltpu.VMEM(ocean.shape, f32)),
            in_specs=[pl.BlockSpec(memory_space=pl.ANY)] * 8,
            out_specs=(
                pl.BlockSpec(memory_space=pltpu.VMEM),
                pl.BlockSpec(memory_space=pltpu.VMEM),
            ),
            scratch_shapes=[
                pltpu.VMEM((6, *padded), f32),
                pltpu.VMEM((6, *padded), f32),
                pltpu.VMEM((3, *padded), f32),
                pltpu.VMEM((3, *padded), f32),
                pltpu.VMEM((3, *padded), f32),
                pltpu.VMEM(cube, f32),
                pltpu.VMEM(cube, f32),
                pltpu.VMEM(cube, f32),
                pltpu.VMEM((STEPS + 1, 3, *TILE), f32),
                pltpu.VMEM(TILE, f32),
                pltpu.VMEM(TILE, jnp.int32),
                pltpu.VMEM(TILE, jnp.int32),
                pltpu.VMEM((STEPS, *TILE), f32),
                pltpu.VMEM((STEPS, 3, *cube), f32),
                pltpu.VMEM((STEPS, 3, *cube), f32),
                pltpu.VMEM((STEPS, chunks, 3, *TILE), f32),
                pltpu.VMEM((STEPS, 5, *TILE), f32),
                pltpu.VMEM((STEPS, *TILE), f32),
                pltpu.VMEM((STEPS, 3, *cube), f32),
                pltpu.VMEM((STEPS, 3, *cube), f32),
                pltpu.VMEM(cube, f32),
                pltpu.VMEM((STEPS, 2, chunks, 2, *TILE), f32),
                pltpu.VMEM((STEPS, 4, chunks, *TILE), f32),
                pltpu.VMEM((STEPS, 5, *TILE), f32),
                pltpu.VMEM((STEPS, 2, *TILE), f32),
                pltpu.VMEM((STEPS, 4, *TILE), f32),
                pltpu.VMEM((3, *cube), f32),
                pltpu.VMEM((STEPS, chunks, *TILE), f32),
                dma((9,)),
                dma((STEPS, 2, 2, 2)),
                dma((STEPS, 2, 2, 2, chunks)),
                dma((2,)),
                dma((2,)),
                dma((STEPS, 2)),
                dma((STEPS, 2, chunks)),
                dma((STEPS, 4)),
                dma((STEPS, 4, chunks)),
                dma((STEPS, 2)),
                dma((STEPS, 2)),
                dma((STEPS, 2)),
                dma((STEPS, 2)),
                dma((STEPS, 4)),
                dma((STEPS, 4)),
            ],
            compiler_params=pltpu.CompilerParams(
                collective_id=0, has_side_effects=True, vmem_limit_bytes=60 << 20
            ),
            name="waves",
        )(*arrays)
        return pl.pallas_call(
            hand_on,
            out_shape=(
                jax.ShapeDtypeStruct(fields.shape, f32),
                jax.ShapeDtypeStruct(ocean.shape, f32),
            ),
            in_specs=[pl.BlockSpec(memory_space=pltpu.VMEM)] * 2,
            out_specs=(pl.BlockSpec(memory_space=pl.ANY), pl.BlockSpec(memory_space=pl.ANY)),
            scratch_shapes=[dma((2,))],
            compiler_params=pltpu.CompilerParams(vmem_limit_bytes=12 << 20),
            name="hand_on",
        )(waves, sea)

    flat = P("gy", "gx")
    deep = P(None, "gy", "gx")
    in_specs = (P(None, None, "gy", "gx"), deep, deep, deep, deep, flat, flat, flat)
    out_specs = (P(None, None, "gy", "gx"), deep)
    return jax.shard_map(local, mesh=mesh, in_specs=in_specs, out_specs=out_specs, check_vma=False)
```

time: 323 us -> 27.8 us (0.09)
  the two profiles are of different devices: /device:TPU:18 before, /device:TPU:27 now
where the time goes in v3:
time: 27.8 us; the launch traced here: 27.7 us
  Pallas kernels  27 us (97%)
  between operations  0.64 us (2%)
    pallas_call x1, Pallas kernels, local(): pl.pallas_call(functools.partial(kernel, counts), out_shape=(pltpu.VMEM(f...  26 us
    pallas_call x1, Pallas kernels, local(): pl.pallas_call(hand_on, out_shape=(jax.ShapeDtypeStruct(fields.shape, f32...  1.03 us

profile of v3, /device:TPU:27, one launch (start us, length us, event | category | flops | bytes accessed | tf_op | source)
XLA Modules:
  0.0 27.7 jit_solution(2281912101837089287)
XLA Ops:
  0.6 26.0 %waves.1 = (f32[9,32,8,128]{3,2,1,0:T(8,128)S(1)}, f32[3,8,128]{2,1,0:T(8,128)S(1)}) custom-call(f32[9,32,8,128]{3,2,1,0:T(8,128)} %fields_ref.1, f32[32,8,128]{2,1,0:T(8,128)} %lame_ref.1, f32[32,8,128]{2,1,0:T(8,128)} %shear_ref.1, f32[32,8,128]{2,1,0:T(8,128)} %buoy_ref.1, f32[3,8,128]{2,1,0:T(8,128)} %ocean_ref.1, f32[8,128]{1,0:T(8,128)} %depth_ref.1, ...), custom_call_target="tpu_custom_call" | custom-call | tf_op jit(solution)/shard_map/waves/pallas_call | solution.py:703
  26.6 1.0 %hand_on.1 = (f32[9,32,8,128]{3,2,1,0:T(8,128)}, f32[3,8,128]{2,1,0:T(8,128)}) custom-call(f32[9,32,8,128]{3,2,1,0:T(8,128)S(1)} %get-tuple-element.4.waves, f32[3,8,128]{2,1,0:T(8,128)S(1)} %get-tuple-element.5.sea), custom_call_target="tpu_custom_call" | custom-call | tf_op jit(solution)/shard_map/hand_on/pallas_call | solution.py:761

commit v4 on v3

--- a/solution.py
+++ b/solution.py
@@ -42,9 +42,8 @@
     wet_ref,
     wave_out,
     ocean_out,
-    stress_a,
+    given,
     stress_b,
-    speed_a,
     speed_b,
     speed_c,
     lame,
@@ -70,21 +69,16 @@
     halo_od,
     speed_rows,
     speed_cols,
+    cols_o,
+    seafloor,
+    sized,
     load_sem,
     send_y,
     recv_y,
-    send_b,
-    recv_b,
     send_x,
     recv_x,
     send_d,
     recv_d,
-    send_oy,
-    recv_oy,
-    send_ox,
-    recv_ox,
-    send_od,
-    recv_od,
 ):
     count_x, count_y = counts
     at_x, at_y = lax.axis_index("gx"), lax.axis_index("gy")
@@ -104,6 +98,13 @@
         for direction, there in enumerate(inside):
             pl.when(there)(functools.partial(act, direction))
 
+    def when(condition, act):
+        if isinstance(condition, bool):
+            if condition:
+                act()
+        else:
+            pl.when(condition)(act)
+
     from_x = inside_x[::-1]
     from_y = inside_y[::-1]
     from_d = inside_d[::-1]
@@ -115,23 +116,23 @@
             lambda d, to=to: pl.semaphore_signal(barrier, inc=1, device_id=to[d]),
         )
 
-    loads = []
-
-    def load(source, target):
-        copy = pltpu.make_async_copy(source, target, load_sem.at[len(loads)])
-        copy.start()
-        loads.append(copy)
+    def rows_done(count, semaphore):
+        part = sized.at[pl.ds(0, count)]
+        pltpu.make_async_copy(part, part, semaphore).wait()
 
     inner_layers = pl.ds(2, layers)
-    load(fields_ref.at[pl.ds(3, 6)], stress_a.at[:, inner_layers])
-    load(fields_ref.at[pl.ds(0, 3)], speed_a.at[:, inner_layers])
-    load(buoy_ref, buoy.at[pl.ds(0, layers)])
-    load(ocean_ref, sea.at[0])
-    load(depth_ref, depth)
-    load(index_ref, index)
-    load(wet_ref, wet_i)
-    load(lame_ref, lame)
-    load(shear_ref, shear)
+    for source, target, place in (
+        (fields_ref, given.at[:, inner_layers], 0),
+        (buoy_ref, buoy, 1),
+        (ocean_ref, sea.at[0], 2),
+        (depth_ref, depth, 2),
+        (index_ref, index, 2),
+        (wet_ref, wet_i, 2),
+        (lame_ref, lame, 3),
+        (shear_ref, shear, 3),
+    ):
+        pltpu.make_async_copy(source, target, load_sem.at[place]).start()
+    stress_a, speed_a = given.at[pl.ds(3, 6)], given.at[pl.ds(0, 3)]
 
     none = jnp.zeros(TILE, jnp.float32)
     row_at = lax.broadcasted_iota(jnp.int32, TILE, 0)
@@ -146,6 +147,9 @@
     wrap_ahead = jnp.logical_or(row_at < 1, row_at >= 6)
     wrap_rows = (wrap_back, wrap_ahead, wrap_back)
 
+    for step in range(STEPS):
+        for item in range(3):
+            seafloor[step, item] = none
     margins = (0, 1, layers + 2, layers + 3)
     for z in margins:
         for field in (XZ, YZ, ZZ):
@@ -158,54 +162,61 @@
     wrap_parts = ((pl.ds(0, 2), (pl.ds(0, 2), pl.ds(7, 1))), (pl.ds(2, 1), (pl.ds(0, 1), pl.ds(6, 2))))
     push_parts = ((pl.ds(0, 2), (pl.ds(7, 1), pl.ds(0, 2))), (pl.ds(2, 1), (pl.ds(6, 2), pl.ds(0, 1))))
 
-    def layers_of(chunk):
-        return pl.ds(0, layers) if chunk is None else pl.ds(chunk * CHUNK, CHUNK)
-
-    def rows_copies(step, direction, chunk, which):
-        source, target = ((wraps, halo_wraps), (pushed, halo_pushed))[which]
+    def rows_copies(step, direction, chunk):
         result = []
-        for part, (fields, rows) in enumerate((wrap_parts, push_parts)[which]):
-            box = (step, fields, layers_of(chunk), rows[direction], slice(None))
+        span = pl.ds(chunk * CHUNK, CHUNK)
+
+        def add(source, target):
             result.append(
                 pltpu.make_async_remote_copy(
-                    source.at[box],
-                    target.at[box],
-                    send_y.at[step, direction, which, part],
-                    recv_y.at[step, direction, which, part, 0 if chunk is None else chunk],
+                    source,
+                    target,
+                    send_y.at[direction],
+                    recv_y.at[step, direction, chunk],
                     device_id=to_y[direction],
                 )
             )
+
+        for source, target, parts in (
+            (wraps, halo_wraps, wrap_parts),
+            (pushed, halo_pushed, push_parts),
+        ):
+            for fields, rows in parts:
+                box = (step, fields, span, rows[direction], slice(None))
+                add(source.at[box], target.at[box])
+        if step == 0:
+            box = (span, pl.ds(6, 2) if direction == 0 else pl.ds(0, 2), slice(None))
+            add(buoy_ref.at[box], halo_buoy.at[box])
         return result
 
-    def buoy_copy(direction):
-        rows = pl.ds(6, 2) if direction == 0 else pl.ds(0, 2)
+    def rows_arrive(step, chunk):
+        count = (11 if step == 0 else 9) * CHUNK + (5 if isinstance(chunk, int) and chunk == 1 else 0)
+        each(from_y, lambda d: rows_done(count, recv_y.at[step, d, chunk]))
+
+    def columns_arrive(step, half):
+        count = 32 + (8 if half == 0 else 0)
+        each(from_x, lambda d: rows_done(count, recv_x.at[step, d, half]))
+
+    def corners_arrive(step, half):
+        count = 8 + (8 if half == 0 else 0)
+        each(from_d, lambda d: rows_done(count, recv_d.at[step, d, half]))
+
+    def columns_copy(step, direction, half):
         return pltpu.make_async_remote_copy(
-            buoy_ref.at[:, rows, :],
-            halo_buoy.at[:, rows, :],
-            send_b.at[direction],
-            recv_b.at[direction],
-            device_id=to_y[direction],
-        )
-
-    def chunk_at(chunk):
-        return pl.ds(0, chunks) if chunk is None else pl.ds(chunk, 1)
-
-    def columns_copy(step, direction, chunk):
-        return pltpu.make_async_remote_copy(
-            packs.at[step, chunk_at(chunk), pl.ds(0, 2)],
-            halo_x.at[step, direction, chunk_at(chunk)],
-            send_x.at[step, direction],
-            recv_x.at[step, direction, 0 if chunk is None else chunk],
+            packs.at[step, pl.ds(2 * half, 2), pl.ds(0, 2)],
+            halo_x.at[step, direction, pl.ds(2 * half, 2)],
+            send_x.at[direction],
+            recv_x.at[step, direction, half],
             device_id=to_x[direction],
         )
 
-    def corner_copy(step, corner, chunk):
+    def corner_copy(step, corner, half):
         rows = pl.ds(4, 4) if corner % 2 == 0 else pl.ds(0, 4)
         return pltpu.make_async_remote_copy(
-            packs.at[step, chunk_at(chunk), 2, rows, :],
-            halo_d.at[step, corner, chunk_at(chunk), rows, :],
-            send_d.at[step, corner],
-            recv_d.at[step, corner, 0 if chunk is None else chunk],
+            packs.at[step, pl.ds(2 * half, 2), 2, rows, :],
+            halo_d.at[step, corner, pl.ds(2 * half, 2), rows, :],
+            send_d.at[corner],
+            recv_d.at[step, corner, half],
             device_id=to_d[corner],
         )
 
@@ -214,8 +225,8 @@
         return pltpu.make_async_remote_copy(
             rows_o.at[step, :, row, :],
             halo_oy.at[step, :, row, :],
-            send_oy.at[step, direction],
-            recv_oy.at[step, direction],
+            send_y.at[direction],
+            recv_y.at[step, direction, 1],
             device_id=to_y[direction],
         )
 
@@ -223,8 +234,8 @@
         return pltpu.make_async_remote_copy(
             packs_o.at[step],
             halo_ox.at[step, direction],
-            send_ox.at[step, direction],
-            recv_ox.at[step, direction],
+            send_x.at[direction],
+            recv_x.at[step, direction, 0],
             device_id=to_x[direction],
         )
 
@@ -232,53 +243,44 @@
         return pltpu.make_async_remote_copy(
             packs_o.at[step],
             halo_od.at[step, corner],
-            send_od.at[step, corner],
-            recv_od.at[step, corner],
+            send_d.at[corner],
+            recv_d.at[step, corner, 0],
             device_id=to_d[corner],
         )
 
     def start_chunk(step, chunk):
+        first = chunk == 1
+
         def start_rows(direction):
-            for which in range(2):
-                for copy in rows_copies(step, direction, chunk, which):
-                    copy.start()
+            for copy in rows_copies(step, direction, chunk):
+                copy.start()
+            when(first, lambda: ocean_rows(step, direction).start())
 
         each(inside_y, start_rows)
-        each(inside_d, lambda d: corner_copy(step, d, chunk).start())
-        each(inside_x, lambda d: columns_copy(step, d, chunk).start())
-
-    def start_ocean(step):
-        each(inside_y, lambda d: ocean_rows(step, d).start())
-        each(inside_d, lambda d: ocean_corner(step, d).start())
-        each(inside_x, lambda d: ocean_columns(step, d).start())
-
-    def wait_rows(step, chunk, which):
-        def wait(direction):
-            for copy in rows_copies(step, direction, chunk, which):
-                copy.wait_recv()
-
-        each(from_y, wait)
-
-    def drain(step):
-        def rows(direction):
-            for which in range(2):
-                for copy in rows_copies(step, direction, None, which):
-                    copy.wait_send()
-            ocean_rows(step, direction).wait_send()
-            if step == 0:
-                buoy_copy(direction).wait_send()
-
-        def corner(d):
-            corner_copy(step, d, None).wait_send()
-            ocean_corner(step, d).wait_send()
-
-        def columns(direction):
-            columns_copy(step, direction, None).wait_send()
-            ocean_columns(step, direction).wait_send()
-
-        each(inside_y, rows)
-        each(inside_d, corner)
-        each(inside_x, columns)
+
+        def start_half():
+            half = chunk // 2 if isinstance(chunk, int) else lax.div(chunk, 2)
+
+            def start_corner(corner):
+                corner_copy(step, corner, half).start()
+                when(first, lambda: ocean_corner(step, corner).start())
+
+            def start_columns(direction):
+                columns_copy(step, direction, half).start()
+                when(first, lambda: ocean_columns(step, direction).start())
+
+            each(inside_d, start_corner)
+            each(inside_x, start_columns)
+
+        when(chunk % 2 == 1 if isinstance(chunk, int) else lax.rem(chunk, 2) == 1, start_half)
+
+    def drain():
+        rows_y = STEPS * (9 * layers + 5) + 2 * layers
+        rows_x = STEPS * (2 * chunks + 1) * 8
+        rows_d = STEPS * (4 * chunks + 8)
+        each(inside_y, lambda d: rows_done(rows_y, send_y.at[d]))
+        each(inside_d, lambda d: rows_done(rows_d, send_d.at[d]))
+        each(inside_x, lambda d: rows_done(rows_x, send_x.at[d]))
 
     def clear_rows(direction):
         first = direction == 0
@@ -400,11 +402,13 @@
         )
 
     def push_chunk(step, chunk, stress, speed):
-        edge_push, edge_x, edge_y = none, none, none
+        edge_push = none if step == 0 else packs[0, chunk, 0]
+        edge_x, edge_y = none, none
         for inner in range(CHUNK):
             z = chunk * CHUNK + inner
             rate = courant * buoy[z]
-            edge_push = packed(edge_push, rate, 3 * CHUNK + inner)
+            if step == 0:
+                edge_push = packed(edge_push, rate, 3 * CHUNK + inner)
             for axis in range(3):
                 tile_x, tile_y = stress[ALONG_X[axis][0], z + 2], stress[ALONG_Y[axis][0], z + 2]
                 kept, wrap = circular_y(tile_y, ALONG_Y[axis][1])
@@ -433,6 +437,7 @@
         packs[step, chunk, 2] = jnp.where(edge_rows, wrap_x, turned(wrap_y, 4, 0))
 
     def join_chunk(step, chunk, speed):
+        floor = none
         side = jnp.where(low_slot, halo_x[step, 1, chunk, 1], halo_x[step, 0, chunk, 1])
         for inner in range(CHUNK):
             z = chunk * CHUNK + inner
@@ -443,8 +448,11 @@
                 )
                 new = pushed[step, FIELD[axis], z] + rate * added
                 speed[axis, z + 2] = new
+                if axis == 2:
+                    floor = floor + jnp.where(index[...] == z, new, 0.0)
                 if step == STEPS - 1:
                     wave_out[axis, z] = new
+        seafloor[step, 0] = seafloor[step, 0] + floor
 
     def corners(step, chunk):
         def of(dx):
@@ -477,11 +485,14 @@
 
     def stress_chunk(step, chunk, speed, stress_old, stress_new):
         side = speed_cols[step, chunk]
+        floor_rows, floor_cols = none, none
         for inner in range(CHUNK):
             z = chunk * CHUNK + inner
             vx, vy, vz = speed[0, z + 2], speed[1, z + 2], speed[2, z + 2]
             hx = [unpacked(side, axis * CHUNK + inner) for axis in range(3)]
             hy = [speed_rows[axis, z] for axis in range(3)]
+            floor_rows = floor_rows + jnp.where(halo_oy[step, 4] == z, hy[2], 0.0)
+            floor_cols = floor_cols + jnp.where(cols_o[step, 4] == z, hx[2], 0.0)
             strain_x = differ(vx, hx[0], 1, False)
             strain_y = differ(vy, hy[1], 0, False)
             strain_z = differ_z(speed, 2, z, False)
@@ -505,6 +516,8 @@
                     wave_out[3 + field, z] = value
                 else:
                     stress_new[field, z + 2] = value
+        seafloor[step, 1] = seafloor[step, 1] + floor_rows
+        seafloor[step, 2] = seafloor[step, 2] + floor_cols
 
     def centred(tile, halo, axis):
         return 0.5 * (shifted(tile, halo, axis, -1) - shifted(tile, halo, axis, 1))
@@ -535,75 +548,45 @@
             pack = packed(pack, item, place)
         packs_o[step] = pack
 
-    def ocean_edge(step):
-        return jnp.where(low_slot, halo_ox[step, 0], halo_ox[step, 1])
-
-    def ocean_level(step, speed):
+    def ocean_level(step):
         level, flux_x, flux_y = sea[step, 0], sea[step, 1], sea[step, 2]
         wet = wet_i[...].astype(jnp.float32)
-        seafloor = none
-        for z in range(layers // 2):
-            seafloor = seafloor + jnp.where(index[...] == z, speed[2, z + 2], 0.0)
-        spread = centred(flux_x, unpacked(ocean_edge(step), 0), 1) + centred(
-            flux_y, halo_oy[step, 1], 0
-        )
-        level = level + wet * (uplift * seafloor - ocean_rate * spread)
+        edge = jnp.where(low_slot, halo_ox[step, 0], halo_ox[step, 1])
+        cols = [unpacked(edge, item) for item in range(5)]
+        for item in range(5):
+            cols_o[step, item] = cols[item]
+        spread = centred(flux_x, cols[0], 1) + centred(flux_y, halo_oy[step, 1], 0)
+        level = level + wet * (uplift * seafloor[step, 0] - ocean_rate * spread)
         sea[step + 1, 0] = level
         press[step] = loading * (wet * level)
 
     def ocean_flux(step):
         level, flux_x, flux_y = sea[step + 1, 0], sea[step, 1], sea[step, 2]
         wet = wet_i[...].astype(jnp.float32)
-        edge = ocean_edge(step)
 
         def of(dx):
             return jnp.where(upper, halo_od[step, 2 * dx + 1], halo_od[step, 2 * dx])
 
         corner = jnp.where(low_slot, of(0), of(1))
 
-        index_rows = halo_oy[step, 4]
-        seafloor = none
-        for z in range(layers // 2):
-            seafloor = seafloor + jnp.where(index_rows == z, speed_rows[2, z], 0.0)
         spread = centred(none, flux_y, 0) + centred(none, unpacked(corner, 0), 1)
         level_rows = halo_oy[step, 2] + halo_oy[step, 3] * (
-            uplift * seafloor - ocean_rate * spread
-        )
-
-        own = packs_o[step]
-        index_edge = jnp.where(lane_at < 4, turned(edge, -16, 1), 0.0)
-        for by in (4, 8, 16):
-            index_edge = index_edge + turned(index_edge, by, 1)
-        index_edge = turned(index_edge, 8 * CHUNK, 1)
-        total = none
-        for chunk in range(layers // 2 // CHUNK):
-            z_at = chunk * CHUNK + group_at - 2 * CHUNK
-            chosen = jnp.logical_and(
-                index_edge == z_at.astype(jnp.float32), lane_at // (4 * CHUNK) == 2
-            )
-            total = total + jnp.where(chosen, speed_cols[step, chunk], 0.0)
-        total = turned(total, -8 * CHUNK, 1)
-        for by in (16, 8, 4):
-            total = total + turned(total, -by, 1)
-        spread_edge = (
-            jnp.where(slot_at == 1, 0.5 * turned(own, -1, 1), 0.0)
-            - jnp.where(slot_at == 2, 0.5 * turned(own, 1, 1), 0.0)
-            + centred(none, turned(corner, -4, 1), 0)
-        )
-        level_edge = turned(edge, -8, 1) + turned(edge, -12, 1) * (
-            uplift * total - ocean_rate * spread_edge
-        )
-
-        slope_x = centred(level, unpacked(level_edge, 0), 1)
+            uplift * seafloor[step, 1] - ocean_rate * spread
+        )
+        spread = centred(none, flux_x, 1) + centred(none, unpacked(corner, 1), 0)
+        level_cols = cols_o[step, 2] + cols_o[step, 3] * (
+            uplift * seafloor[step, 2] - ocean_rate * spread
+        )
+        slope_x = centred(level, level_cols, 1)
         slope_y = centred(level, level_rows, 0)
-        around_x = around(flux_x, halo_oy[step, 0], unpacked(edge, 0))
-        around_y = around(flux_y, halo_oy[step, 1], unpacked(edge, 1))
+        around_x = around(flux_x, halo_oy[step, 0], cols_o[step, 0])
+        around_y = around(flux_y, halo_oy[step, 1], cols_o[step, 1])
         pull = ocean_rate * depth[...]
         sea[step + 1, 1] = wet * (flux_x - pull * slope_x + viscous * around_x)
         sea[step + 1, 2] = wet * (flux_y - pull * slope_y + viscous * around_y)
 
-    for copy in loads[:7]:
-        copy.wait()
+    for count, place in ((9 * 8 * layers, 0), (8 * layers, 1), (6 * 8, 2)):
+        rows_done(count, load_sem.at[place])
     speeds = (speed_a, speed_b, speed_c)
     stresses = (stress_a, stress_b, stress_b)
 
@@ -611,72 +594,72 @@
         push_chunk(0, chunk, stress_a, speed_a)
         return carry
 
-    lax.fori_loop(0, chunks, first_push, 0)
+    lax.fori_loop(0, 2, first_push, 0)
     ocean_prepare(0)
 
     peers = sum(there.astype(jnp.int32) for there in (*inside_x, *inside_y, *inside_d))
     pl.semaphore_wait(barrier, peers)
+
+    def paced(chunk, carry):
+        start_chunk(0, chunk - 2)
+        push_chunk(0, chunk, stress_a, speed_a)
+        return carry
 
     def first_send(chunk, carry):
         start_chunk(0, chunk)
         return carry
 
-    start_chunk(0, 0)
-    each(inside_y, lambda d: buoy_copy(d).start())
-    start_ocean(0)
-    lax.fori_loop(1, chunks, first_send, 0)
-    for copy in loads[7:]:
-        copy.wait()
+    lax.fori_loop(2, chunks, paced, 0)
+    lax.fori_loop(chunks - 2, chunks, first_send, 0)
+    rows_done(2 * 8 * layers, load_sem.at[3])
 
     for step in range(STEPS):
         last = step == STEPS - 1
         speed_old, speed_new = speeds[step], speeds[step + 1]
         stress_old, stress_new = stresses[step], stresses[step + 1]
 
+        def stress_of(chunk):
+            halo_chunk(step, chunk)
+            stress_chunk(step, chunk, speed_new, stress_old, stress_new)
+
+        def push_of(chunk):
+            if not last:
+                push_chunk(step + 1, chunk, stress_new, speed_new)
+                start_chunk(step + 1, chunk)
+
+        columns_arrive(step, 0)
+        rows_arrive(step, 0)
+        join_chunk(step, 0, speed_new)
+        rows_arrive(step, 1)
+        corners_arrive(step, 0)
+        join_chunk(step, 1, speed_new)
+        ocean_level(step)
+        stress_of(0)
+        columns_arrive(step, 1)
+
         def body(turn, carry):
-            @pl.when(turn < chunks)
-            def _():
-                each(from_x, lambda d: columns_copy(step, d, turn).wait_recv())
-                wait_rows(step, turn, 0)
-                join_chunk(step, turn, speed_new)
-
-            @pl.when(turn == 1)
-            def _():
-                each(from_x, lambda d: ocean_columns(step, d).wait_recv())
-                each(from_y, lambda d: ocean_rows(step, d).wait_recv())
-                ocean_level(step, speed_new)
-                if step == 0:
-                    each(from_y, lambda d: buoy_copy(d).wait_recv())
-
-            @pl.when(jnp.logical_and(turn >= 1, turn <= chunks))
-            def _():
-                wait_rows(step, turn - 1, 1)
-                each(from_d, lambda d: corner_copy(step, d, turn - 1).wait_recv())
-                halo_chunk(step, turn - 1)
-                stress_chunk(step, turn - 1, speed_new, stress_old, stress_new)
+            rows_arrive(step, turn)
+            pl.when(turn == 3)(lambda: corners_arrive(step, 1))
+            join_chunk(step, turn, speed_new)
+            stress_of(turn - 1)
+            push_of(turn - 2)
 
             @pl.when(turn == 2)
             def _():
-                each(from_d, lambda d: ocean_corner(step, d).wait_recv())
                 ocean_flux(step)
                 if not last:
                     ocean_prepare(step + 1)
-                    start_ocean(step + 1)
-
-            if not last:
-
-                @pl.when(turn >= 2)
-                def _():
-                    push_chunk(step + 1, turn - 2, stress_new, speed_new)
-                    start_chunk(step + 1, turn - 2)
 
             return carry
 
-        lax.fori_loop(0, chunks + (1 if last else 2), body, 0)
-        drain(step)
+        lax.fori_loop(2, chunks, body, 0)
+        stress_of(chunks - 1)
+        push_of(chunks - 2)
+        push_of(chunks - 1)
 
     for item in range(3):
         ocean_out[item] = sea[STEPS, item]
+    drain()
 
 
 def hand_on(waves, sea, waves_out, sea_out, sem):
@@ -709,9 +692,8 @@
                 pl.BlockSpec(memory_space=pltpu.VMEM),
             ),
             scratch_shapes=[
+                pltpu.VMEM((9, *padded), f32),
                 pltpu.VMEM((6, *padded), f32),
-                pltpu.VMEM((6, *padded), f32),
-                pltpu.VMEM((3, *padded), f32),
                 pltpu.VMEM((3, *padded), f32),
                 pltpu.VMEM((3, *padded), f32),
                 pltpu.VMEM(cube, f32),
@@ -737,21 +719,16 @@
                 pltpu.VMEM((STEPS, 4, *TILE), f32),
                 pltpu.VMEM((3, *cube), f32),
                 pltpu.VMEM((STEPS, chunks, *TILE), f32),
-                dma((9,)),
-                dma((STEPS, 2, 2, 2)),
-                dma((STEPS, 2, 2, 2, chunks)),
+                pltpu.VMEM((STEPS, 5, *TILE), f32),
+                pltpu.VMEM((STEPS, 3, *TILE), f32),
+                pltpu.VMEM((9 * layers * 8, 128), f32),
+                dma((4,)),
                 dma((2,)),
+                dma((STEPS, 2, chunks)),
                 dma((2,)),
-                dma((STEPS, 2)),
-                dma((STEPS, 2, chunks)),
-                dma((STEPS, 4)),
-                dma((STEPS, 4, chunks)),
-                dma((STEPS, 2)),
-                dma((STEPS, 2)),
-                dma((STEPS, 2)),
-                dma((STEPS, 2)),
-                dma((STEPS, 4)),
-                dma((STEPS, 4)),
+                dma((STEPS, 2, chunks // 2)),
+                dma((4,)),
+                dma((STEPS, 4, chunks // 2)),
             ],
             compiler_params=pltpu.CompilerParams(
                 collective_id=0, has_side_effects=True, vmem_limit_bytes=60 << 20

time: 27.8 us -> 25.9 us (0.932)
  Pallas kernels: 27 us -> 25.2 us
    pallas_call x1, Pallas kernels: 26 us -> 24.1 us  [local(): pl.pallas_call(functools.partial(kernel, counts), out_shape=(pltpu.VMEM(f...]
where the time goes in v4:
time: 25.9 us; the launch traced here: 25.8 us
  Pallas kernels  25.2 us (97%)
  between operations  0.64 us (2%)
    pallas_call x1, Pallas kernels, local(): pl.pallas_call(functools.partial(kernel, counts), out_shape=(pltpu.VMEM(f...  24.1 us
    pallas_call x1, Pallas kernels, local(): pl.pallas_call(hand_on, out_shape=(jax.ShapeDtypeStruct(fields.shape, f32...  1.03 us

profile of v4, /device:TPU:27, one launch (start us, length us, event | category | flops | bytes accessed | tf_op | source)
XLA Modules:
  0.0 25.8 jit_solution(8954631641060340181)
XLA Ops:
  0.6 24.1 %waves.1 = (f32[9,32,8,128]{3,2,1,0:T(8,128)S(1)}, f32[3,8,128]{2,1,0:T(8,128)S(1)}) custom-call(f32[9,32,8,128]{3,2,1,0:T(8,128)} %fields_ref.1, f32[32,8,128]{2,1,0:T(8,128)} %lame_ref.1, f32[32,8,128]{2,1,0:T(8,128)} %shear_ref.1, f32[32,8,128]{2,1,0:T(8,128)} %buoy_ref.1, f32[3,8,128]{2,1,0:T(8,128)} %ocean_ref.1, f32[8,128]{1,0:T(8,128)} %depth_ref.1, ...), custom_call_target="tpu_custom_call" | custom-call | tf_op jit(solution)/shard_map/waves/pallas_call | solution.py:686
  24.8 1.0 %hand_on.1 = (f32[9,32,8,128]{3,2,1,0:T(8,128)}, f32[3,8,128]{2,1,0:T(8,128)}) custom-call(f32[9,32,8,128]{3,2,1,0:T(8,128)S(1)} %get-tuple-element.4.waves, f32[3,8,128]{2,1,0:T(8,128)S(1)} %get-tuple-element.5.sea), custom_call_target="tpu_custom_call" | custom-call | tf_op jit(solution)/shard_map/hand_on/pallas_call | solution.py:738

commit v5 on v4

--- a/solution.py
+++ b/solution.py
@@ -8,7 +8,8 @@
 from jax.sharding import PartitionSpec as P
 
 STEPS = 2
-CHUNK = 8
+CHUNK = 4
+PACK = 8
 TILE = (8, 128)
 
 near = 9.0 / 8.0
@@ -71,6 +72,7 @@
     speed_cols,
     cols_o,
     seafloor,
+    edges,
     sized,
     load_sem,
     send_y,
@@ -84,6 +86,7 @@
     at_x, at_y = lax.axis_index("gx"), lax.axis_index("gy")
     layers = fields_ref.shape[1]
     chunks = layers // CHUNK
+    pairs = layers // PACK
 
     next_x = (jnp.minimum(at_x + 1, count_x - 1), jnp.maximum(at_x - 1, 0))
     next_y = (jnp.minimum(at_y + 1, count_y - 1), jnp.maximum(at_y - 1, 0))
@@ -190,16 +193,16 @@
         return result
 
     def rows_arrive(step, chunk):
-        count = (11 if step == 0 else 9) * CHUNK + (5 if isinstance(chunk, int) and chunk == 1 else 0)
+        count = (11 if step == 0 else 9) * CHUNK + (5 if isinstance(chunk, int) and chunk == 3 else 0)
         each(from_y, lambda d: rows_done(count, recv_y.at[step, d, chunk]))
 
     def columns_arrive(step, half):
-        count = 32 + (8 if half == 0 else 0)
+        count = 32 + (8 if half == 1 else 0)
         each(from_x, lambda d: rows_done(count, recv_x.at[step, d, half]))
 
-    def corners_arrive(step, half):
-        count = 8 + (8 if half == 0 else 0)
-        each(from_d, lambda d: rows_done(count, recv_d.at[step, d, half]))
+    def corners_arrive(step, pair):
+        count = 12 if pair == 1 else 4
+        each(from_d, lambda d: rows_done(count, recv_d.at[step, d, pair]))
 
     def columns_copy(step, direction, half):
         return pltpu.make_async_remote_copy(
@@ -210,13 +213,13 @@
             device_id=to_x[direction],
         )
 
-    def corner_copy(step, corner, half):
+    def corner_copy(step, corner, pair):
         rows = pl.ds(4, 4) if corner % 2 == 0 else pl.ds(0, 4)
         return pltpu.make_async_remote_copy(
-            packs.at[step, pl.ds(2 * half, 2), 2, rows, :],
-            halo_d.at[step, corner, pl.ds(2 * half, 2), rows, :],
+            packs.at[step, pair, 2, rows, :],
+            halo_d.at[step, corner, pair, rows, :],
             send_d.at[corner],
-            recv_d.at[step, corner, half],
+            recv_d.at[step, corner, pair],
             device_id=to_d[corner],
         )
 
@@ -226,7 +229,7 @@
             rows_o.at[step, :, row, :],
             halo_oy.at[step, :, row, :],
             send_y.at[direction],
-            recv_y.at[step, direction, 1],
+            recv_y.at[step, direction, 3],
             device_id=to_y[direction],
         )
 
@@ -235,7 +238,7 @@
             packs_o.at[step],
             halo_ox.at[step, direction],
             send_x.at[direction],
-            recv_x.at[step, direction, 0],
+            recv_x.at[step, direction, 1],
             device_id=to_x[direction],
         )
 
@@ -244,40 +247,39 @@
             packs_o.at[step],
             halo_od.at[step, corner],
             send_d.at[corner],
-            recv_d.at[step, corner, 0],
+            recv_d.at[step, corner, 1],
             device_id=to_d[corner],
         )
 
     def start_chunk(step, chunk):
-        first = chunk == 1
-
         def start_rows(direction):
             for copy in rows_copies(step, direction, chunk):
                 copy.start()
-            when(first, lambda: ocean_rows(step, direction).start())
+            when(chunk == 3, lambda: ocean_rows(step, direction).start())
 
         each(inside_y, start_rows)
 
-        def start_half():
-            half = chunk // 2 if isinstance(chunk, int) else lax.div(chunk, 2)
-
-            def start_corner(corner):
-                corner_copy(step, corner, half).start()
-                when(first, lambda: ocean_corner(step, corner).start())
-
-            def start_columns(direction):
+    def start_pair(step, pair):
+        def start_corner(corner):
+            corner_copy(step, corner, pair).start()
+            when(pair == 1, lambda: ocean_corner(step, corner).start())
+
+        def start_columns(half):
+            def start(direction):
                 columns_copy(step, direction, half).start()
-                when(first, lambda: ocean_columns(step, direction).start())
-
-            each(inside_d, start_corner)
-            each(inside_x, start_columns)
-
-        when(chunk % 2 == 1 if isinstance(chunk, int) else lax.rem(chunk, 2) == 1, start_half)
+                if half == 1:
+                    ocean_columns(step, direction).start()
+
+            each(inside_x, start)
+
+        each(inside_d, start_corner)
+        when(pair == 1, lambda: start_columns(0))
+        when(pair == 3, lambda: start_columns(1))
 
     def drain():
         rows_y = STEPS * (9 * layers + 5) + 2 * layers
-        rows_x = STEPS * (2 * chunks + 1) * 8
-        rows_d = STEPS * (4 * chunks + 8)
+        rows_x = STEPS * (2 * pairs + 1) * 8
+        rows_d = STEPS * (4 * pairs + 8)
         each(inside_y, lambda d: rows_done(rows_y, send_y.at[d]))
         each(inside_d, lambda d: rows_done(rows_d, send_d.at[d]))
         each(inside_x, lambda d: rows_done(rows_x, send_x.at[d]))
@@ -304,15 +306,15 @@
     def clear_columns(direction):
         for step in range(STEPS):
             halo_ox[step, direction] = none
-            for chunk in range(chunks):
+            for pair in range(pairs):
                 for part in range(2):
-                    halo_x[step, direction, chunk, part] = none
+                    halo_x[step, direction, pair, part] = none
 
     def clear_corner(corner):
         for step in range(STEPS):
             halo_od[step, corner] = none
-            for chunk in range(chunks):
-                halo_d[step, corner, chunk] = none
+            for pair in range(pairs):
+                halo_d[step, corner, pair] = none
 
     each(tuple(jnp.logical_not(there) for there in from_y), clear_rows)
     each(tuple(jnp.logical_not(there) for there in from_x), clear_columns)
@@ -401,14 +403,18 @@
             - weight(lane_at >= 2, far) * two
         )
 
-    def push_chunk(step, chunk, stress, speed):
-        edge_push = none if step == 0 else packs[0, chunk, 0]
-        edge_x, edge_y = none, none
+    def push_chunk(step, pair, sub, stress, speed):
+        if sub == 0:
+            edge_push = none if step == 0 else packs[0, pair, 0]
+            edge_x, edge_y = none, none
+        else:
+            edge_push, edge_x, edge_y = packs[step, pair, 0], edges[0], edges[1]
         for inner in range(CHUNK):
-            z = chunk * CHUNK + inner
+            place = sub * CHUNK + inner
+            z = pair * PACK + place
             rate = courant * buoy[z]
             if step == 0:
-                edge_push = packed(edge_push, rate, 3 * CHUNK + inner)
+                edge_push = packed(edge_push, rate, 3 * PACK + place)
             for axis in range(3):
                 tile_x, tile_y = stress[ALONG_X[axis][0], z + 2], stress[ALONG_Y[axis][0], z + 2]
                 kept, wrap = circular_y(tile_y, ALONG_Y[axis][1])
@@ -420,31 +426,34 @@
                 push = speed[axis, z + 2] + rate * total
                 pushed[step, FIELD[axis], z] = push
                 wraps[step, FIELD[axis], z] = wrap
-                place = axis * CHUNK + inner
-                edge_push = packed(edge_push, push, place)
-                edge_x = packed(edge_x, tile_x, place)
-                edge_y = packed(edge_y, tile_y, place)
-        first = lane_at < 4 * CHUNK
-        second = jnp.logical_and(lane_at >= 4 * CHUNK, lane_at < 8 * CHUNK)
-        packs[step, chunk, 0] = edge_push
+                edge_push = packed(edge_push, push, axis * PACK + place)
+                edge_x = packed(edge_x, tile_x, axis * PACK + place)
+                edge_y = packed(edge_y, tile_y, axis * PACK + place)
+        packs[step, pair, 0] = edge_push
+        if sub == 0:
+            edges[0], edges[1] = edge_x, edge_y
+            return
+        first = lane_at < 4 * PACK
+        second = jnp.logical_and(lane_at >= 4 * PACK, lane_at < 8 * PACK)
         wrap_x = jnp.where(
             first, wrapped(edge_x, 1, True, *slot_ends), wrapped(edge_x, 1, False, *slot_ends)
         )
-        packs[step, chunk, 1] = wrap_x
+        packs[step, pair, 1] = wrap_x
         wrap_y = jnp.where(
             second, wrapped(edge_y, 0, True, *row_ends), wrapped(edge_y, 0, False, *row_ends)
         )
-        packs[step, chunk, 2] = jnp.where(edge_rows, wrap_x, turned(wrap_y, 4, 0))
-
-    def join_chunk(step, chunk, speed):
+        packs[step, pair, 2] = jnp.where(edge_rows, wrap_x, turned(wrap_y, 4, 0))
+
+    def join_chunk(step, pair, sub, speed):
         floor = none
-        side = jnp.where(low_slot, halo_x[step, 1, chunk, 1], halo_x[step, 0, chunk, 1])
+        side = jnp.where(low_slot, halo_x[step, 1, pair, 1], halo_x[step, 0, pair, 1])
         for inner in range(CHUNK):
-            z = chunk * CHUNK + inner
+            place = sub * CHUNK + inner
+            z = pair * PACK + place
             rate = courant * buoy[z]
             for axis in range(3):
                 added = jnp.where(wrap_rows[axis], halo_wraps[step, FIELD[axis], z], 0.0) + jnp.where(
-                    edge_lanes, unpacked(side, axis * CHUNK + inner), 0.0
+                    edge_lanes, unpacked(side, axis * PACK + place), 0.0
                 )
                 new = pushed[step, FIELD[axis], z] + rate * added
                 speed[axis, z + 2] = new
@@ -454,45 +463,49 @@
                     wave_out[axis, z] = new
         seafloor[step, 0] = seafloor[step, 0] + floor
 
-    def corners(step, chunk):
+    def corners(step, pair):
         def of(dx):
             return jnp.where(
-                upper, halo_d[step, 2 * dx + 1, chunk], halo_d[step, 2 * dx, chunk]
+                upper, halo_d[step, 2 * dx + 1, pair], halo_d[step, 2 * dx, pair]
             )
 
         low, high = of(0), of(1)
         wrap_y = turned(jnp.where(low_slot, low, high), 4, 0)
         return jnp.where(low_slot, high, low), jnp.where(edge_rows, wrap_y, 0.0)
 
-    def halo_chunk(step, chunk):
-        wrap_x, wrap_y = corners(step, chunk)
-        edge = jnp.where(low_slot, halo_x[step, 0, chunk, 0], halo_x[step, 1, chunk, 0])
-        span = lane_at // (4 * CHUNK)
-        rate_edge = jnp.where(
-            span == 0,
-            turned(edge, 4 * CHUNK, 1),
-            jnp.where(span == 1, turned(edge, 8 * CHUNK, 1), turned(edge, 12 * CHUNK, 1)),
-        )
-        speed_cols[step, chunk] = edge + rate_edge * (packs[step, chunk, 1] + wrap_y)
+    def halo_chunk(step, pair, sub):
+        wrap_x, wrap_y = corners(step, pair)
+        if sub == 0:
+            edge = jnp.where(low_slot, halo_x[step, 0, pair, 0], halo_x[step, 1, pair, 0])
+            span = lane_at // (4 * PACK)
+            rate_edge = jnp.where(
+                span == 0,
+                turned(edge, 4 * PACK, 1),
+                jnp.where(span == 1, turned(edge, 8 * PACK, 1), turned(edge, 12 * PACK, 1)),
+            )
+            speed_cols[step, pair] = edge + rate_edge * (packs[step, pair, 1] + wrap_y)
         for inner in range(CHUNK):
-            z = chunk * CHUNK + inner
+            place = sub * CHUNK + inner
+            z = pair * PACK + place
             rate = courant * halo_buoy[z]
             for axis in range(3):
                 added = wraps[step, FIELD[axis], z] + jnp.where(
-                    edge_lanes, unpacked(wrap_x, axis * CHUNK + inner), 0.0
+                    edge_lanes, unpacked(wrap_x, axis * PACK + place), 0.0
                 )
                 speed_rows[axis, z] = halo_pushed[step, FIELD[axis], z] + rate * added
 
-    def stress_chunk(step, chunk, speed, stress_old, stress_new):
-        side = speed_cols[step, chunk]
+    def stress_chunk(step, pair, sub, speed, stress_old, stress_new, pressed):
+        side = speed_cols[step, pair]
         floor_rows, floor_cols = none, none
         for inner in range(CHUNK):
-            z = chunk * CHUNK + inner
+            place = sub * CHUNK + inner
+            z = pair * PACK + place
             vx, vy, vz = speed[0, z + 2], speed[1, z + 2], speed[2, z + 2]
-            hx = [unpacked(side, axis * CHUNK + inner) for axis in range(3)]
+            hx = [unpacked(side, axis * PACK + place) for axis in range(3)]
             hy = [speed_rows[axis, z] for axis in range(3)]
-            floor_rows = floor_rows + jnp.where(halo_oy[step, 4] == z, hy[2], 0.0)
-            floor_cols = floor_cols + jnp.where(cols_o[step, 4] == z, hx[2], 0.0)
+            if pressed:
+                floor_rows = floor_rows + jnp.where(halo_oy[step, 4] == z, hy[2], 0.0)
+                floor_cols = floor_cols + jnp.where(cols_o[step, 4] == z, hx[2], 0.0)
             strain_x = differ(vx, hx[0], 1, False)
             strain_y = differ(vy, hy[1], 0, False)
             strain_z = differ_z(speed, 2, z, False)
@@ -502,22 +515,24 @@
             rate = courant * shear[z]
             bulk = (courant * lame[z]) * (strain_x + strain_y + strain_z)
             twice = 2.0 * rate
-            load_z = jnp.where(index[...] == z, press[step], 0.0)
             new = {
                 XX: stress_old[XX, z + 2] + (bulk + twice * strain_x),
                 YY: stress_old[YY, z + 2] + (bulk + twice * strain_y),
-                ZZ: stress_old[ZZ, z + 2] + (bulk + twice * strain_z) - load_z,
+                ZZ: stress_old[ZZ, z + 2] + (bulk + twice * strain_z),
                 XY: stress_old[XY, z + 2] + rate * shear_xy,
                 XZ: stress_old[XZ, z + 2] + rate * shear_xz,
                 YZ: stress_old[YZ, z + 2] + rate * shear_yz,
             }
+            if pressed:
+                new[ZZ] = new[ZZ] - jnp.where(index[...] == z, press[step], 0.0)
             for field, value in new.items():
                 if step == STEPS - 1:
                     wave_out[3 + field, z] = value
                 else:
                     stress_new[field, z + 2] = value
-        seafloor[step, 1] = seafloor[step, 1] + floor_rows
-        seafloor[step, 2] = seafloor[step, 2] + floor_cols
+        if pressed:
+            seafloor[step, 1] = seafloor[step, 1] + floor_rows
+            seafloor[step, 2] = seafloor[step, 2] + floor_cols
 
     def centred(tile, halo, axis):
         return 0.5 * (shifted(tile, halo, axis, -1) - shifted(tile, halo, axis, 1))
@@ -560,6 +575,20 @@
         sea[step + 1, 0] = level
         press[step] = loading * (wet * level)
 
+    def press_late(step, stress_new):
+        floor_rows, floor_cols = none, none
+        for z in range(2 * CHUNK):
+            edge = unpacked(speed_cols[step, 0], 2 * PACK + z)
+            floor_rows = floor_rows + jnp.where(halo_oy[step, 4] == z, speed_rows[2, z], 0.0)
+            floor_cols = floor_cols + jnp.where(cols_o[step, 4] == z, edge, 0.0)
+            less = jnp.where(index[...] == z, press[step], 0.0)
+            if step == STEPS - 1:
+                wave_out[3 + ZZ, z] = wave_out[3 + ZZ, z] - less
+            else:
+                stress_new[ZZ, z + 2] = stress_new[ZZ, z + 2] - less
+        seafloor[step, 1] = floor_rows
+        seafloor[step, 2] = floor_cols
+
     def ocean_flux(step):
         level, flux_x, flux_y = sea[step + 1, 0], sea[step, 1], sea[step, 2]
         wet = wet_i[...].astype(jnp.float32)
@@ -590,8 +619,9 @@
     speeds = (speed_a, speed_b, speed_c)
     stresses = (stress_a, stress_b, stress_b)
 
-    def first_push(chunk, carry):
-        push_chunk(0, chunk, stress_a, speed_a)
+    def first_push(pair, carry):
+        for sub in range(2):
+            push_chunk(0, pair, sub, stress_a, speed_a)
         return carry
 
     lax.fori_loop(0, 2, first_push, 0)
@@ -600,17 +630,18 @@
     peers = sum(there.astype(jnp.int32) for there in (*inside_x, *inside_y, *inside_d))
     pl.semaphore_wait(barrier, peers)
 
-    def paced(chunk, carry):
-        start_chunk(0, chunk - 2)
-        push_chunk(0, chunk, stress_a, speed_a)
+    def first_send(pair, carry):
+        for sub in range(2):
+            start_chunk(0, 2 * pair + sub)
+        start_pair(0, pair)
         return carry
 
-    def first_send(chunk, carry):
-        start_chunk(0, chunk)
-        return carry
-
-    lax.fori_loop(2, chunks, paced, 0)
-    lax.fori_loop(chunks - 2, chunks, first_send, 0)
+    def paced(pair, carry):
+        first_send(pair - 2, carry)
+        return first_push(pair, carry)
+
+    lax.fori_loop(2, pairs, paced, 0)
+    lax.fori_loop(pairs - 2, pairs, first_send, 0)
     rows_done(2 * 8 * layers, load_sem.at[3])
 
     for step in range(STEPS):
@@ -618,44 +649,51 @@
         speed_old, speed_new = speeds[step], speeds[step + 1]
         stress_old, stress_new = stresses[step], stresses[step + 1]
 
-        def stress_of(chunk):
-            halo_chunk(step, chunk)
-            stress_chunk(step, chunk, speed_new, stress_old, stress_new)
-
-        def push_of(chunk):
+        def join_of(pair, sub):
+            rows_arrive(step, 2 * pair + sub)
+            join_chunk(step, pair, sub, speed_new)
+
+        def stress_of(pair, sub, pressed=True):
+            halo_chunk(step, pair, sub)
+            stress_chunk(step, pair, sub, speed_new, stress_old, stress_new, pressed)
+
+        def push_of(pair, sub):
             if not last:
-                push_chunk(step + 1, chunk, stress_new, speed_new)
-                start_chunk(step + 1, chunk)
+                push_chunk(step + 1, pair, sub, stress_new, speed_new)
+                start_chunk(step + 1, 2 * pair + sub)
+                if sub == 1:
+                    start_pair(step + 1, pair)
 
         columns_arrive(step, 0)
-        rows_arrive(step, 0)
-        join_chunk(step, 0, speed_new)
-        rows_arrive(step, 1)
+        join_of(0, 0)
+        join_of(0, 1)
         corners_arrive(step, 0)
-        join_chunk(step, 1, speed_new)
+        stress_of(0, 0, False)
+        join_of(1, 0)
+        stress_of(0, 1, False)
+        columns_arrive(step, 1)
+        corners_arrive(step, 1)
+        join_of(1, 1)
         ocean_level(step)
-        stress_of(0)
-        columns_arrive(step, 1)
-
-        def body(turn, carry):
-            rows_arrive(step, turn)
-            pl.when(turn == 3)(lambda: corners_arrive(step, 1))
-            join_chunk(step, turn, speed_new)
-            stress_of(turn - 1)
-            push_of(turn - 2)
-
-            @pl.when(turn == 2)
-            def _():
+        press_late(step, stress_new)
+        stress_of(1, 0)
+        push_of(0, 0)
+        push_of(0, 1)
+        for pair in range(2, pairs):
+            join_of(pair, 0)
+            stress_of(pair - 1, 1)
+            push_of(pair - 1, 0)
+            if pair == 2:
                 ocean_flux(step)
                 if not last:
                     ocean_prepare(step + 1)
-
-            return carry
-
-        lax.fori_loop(2, chunks, body, 0)
-        stress_of(chunks - 1)
-        push_of(chunks - 2)
-        push_of(chunks - 1)
+            corners_arrive(step, pair)
+            join_of(pair, 1)
+            stress_of(pair, 0)
+            push_of(pair - 1, 1)
+        stress_of(pairs - 1, 1)
+        push_of(pairs - 1, 0)
+        push_of(pairs - 1, 1)
 
     for item in range(3):
         ocean_out[item] = sea[STEPS, item]
@@ -679,7 +717,7 @@
     def local(*arrays):
         fields, ocean = arrays[0], arrays[4]
         layers = fields.shape[1]
-        chunks = layers // CHUNK
+        chunks, pairs = layers // CHUNK, layers // PACK
         f32, dma = jnp.float32, pltpu.SemaphoreType.DMA
         cube = (layers, *TILE)
         padded = (layers + 4, *TILE)
@@ -706,29 +744,30 @@
                 pltpu.VMEM((STEPS, *TILE), f32),
                 pltpu.VMEM((STEPS, 3, *cube), f32),
                 pltpu.VMEM((STEPS, 3, *cube), f32),
-                pltpu.VMEM((STEPS, chunks, 3, *TILE), f32),
+                pltpu.VMEM((STEPS, pairs, 3, *TILE), f32),
                 pltpu.VMEM((STEPS, 5, *TILE), f32),
                 pltpu.VMEM((STEPS, *TILE), f32),
                 pltpu.VMEM((STEPS, 3, *cube), f32),
                 pltpu.VMEM((STEPS, 3, *cube), f32),
                 pltpu.VMEM(cube, f32),
-                pltpu.VMEM((STEPS, 2, chunks, 2, *TILE), f32),
-                pltpu.VMEM((STEPS, 4, chunks, *TILE), f32),
+                pltpu.VMEM((STEPS, 2, pairs, 2, *TILE), f32),
+                pltpu.VMEM((STEPS, 4, pairs, *TILE), f32),
                 pltpu.VMEM((STEPS, 5, *TILE), f32),
                 pltpu.VMEM((STEPS, 2, *TILE), f32),
                 pltpu.VMEM((STEPS, 4, *TILE), f32),
                 pltpu.VMEM((3, *cube), f32),
-                pltpu.VMEM((STEPS, chunks, *TILE), f32),
+                pltpu.VMEM((STEPS, pairs, *TILE), f32),
                 pltpu.VMEM((STEPS, 5, *TILE), f32),
                 pltpu.VMEM((STEPS, 3, *TILE), f32),
+                pltpu.VMEM((2, *TILE), f32),
                 pltpu.VMEM((9 * layers * 8, 128), f32),
                 dma((4,)),
                 dma((2,)),
                 dma((STEPS, 2, chunks)),
                 dma((2,)),
-                dma((STEPS, 2, chunks // 2)),
+                dma((STEPS, 2, 2)),
                 dma((4,)),
-                dma((STEPS, 4, chunks // 2)),
+                dma((STEPS, 4, pairs)),
             ],
             compiler_params=pltpu.CompilerParams(
                 collective_id=0, has_side_effects=True, vmem_limit_bytes=60 << 20

time: 25.9 us -> 24.9 us (0.961)
  Pallas kernels: 25.2 us -> 24.1 us
    pallas_call x1, Pallas kernels: 24.1 us -> 23.1 us  [local(): pl.pallas_call(functools.partial(kernel, counts), out_shape=(pltpu.VMEM(f...]
where the time goes in v5:
time: 24.9 us; the launch traced here: 24.8 us
  Pallas kernels  24.1 us (97%)
  between operations  0.64 us (3%)
    pallas_call x1, Pallas kernels, local(): pl.pallas_call(functools.partial(kernel, counts), out_shape=(pltpu.VMEM(f...  23.1 us
    pallas_call x1, Pallas kernels, local(): pl.pallas_call(hand_on, out_shape=(jax.ShapeDtypeStruct(fields.shape, f32...  1.03 us

profile of v5, /device:TPU:27, one launch (start us, length us, event | category | flops | bytes accessed | tf_op | source)
XLA Modules:
  0.0 24.8 jit_solution(9855473872344734309)
XLA Ops:
  0.6 23.1 %waves.1 = (f32[9,32,8,128]{3,2,1,0:T(8,128)S(1)}, f32[3,8,128]{2,1,0:T(8,128)S(1)}) custom-call(f32[9,32,8,128]{3,2,1,0:T(8,128)} %fields_ref.1, f32[32,8,128]{2,1,0:T(8,128)} %lame_ref.1, f32[32,8,128]{2,1,0:T(8,128)} %shear_ref.1, f32[32,8,128]{2,1,0:T(8,128)} %buoy_ref.1, f32[3,8,128]{2,1,0:T(8,128)} %ocean_ref.1, f32[8,128]{1,0:T(8,128)} %depth_ref.1, ...), custom_call_target="tpu_custom_call" | custom-call | tf_op jit(solution)/shard_map/waves/pallas_call | solution.py:724
  23.7 1.0 %hand_on.1 = (f32[9,32,8,128]{3,2,1,0:T(8,128)}, f32[3,8,128]{2,1,0:T(8,128)}) custom-call(f32[9,32,8,128]{3,2,1,0:T(8,128)S(1)} %get-tuple-element.4.waves, f32[3,8,128]{2,1,0:T(8,128)S(1)} %get-tuple-element.5.sea), custom_call_target="tpu_custom_call" | custom-call | tf_op jit(solution)/shard_map/hand_on/pallas_call | solution.py:777

commit v6 on v5

--- a/solution.py
+++ b/solution.py
@@ -12,9 +12,8 @@
 PACK = 8
 TILE = (8, 128)
 
-near = 9.0 / 8.0
-far = -1.0 / 24.0
-courant = 0.3
+near = -27.0
+courant = 0.3 * (-1.0 / 24.0)
 ocean_rate = 0.3
 uplift = 0.5
 loading = 0.5
@@ -336,13 +335,13 @@
         after = shifted(tile, halo, axis, -1)
         if forward:
             after_two = shifted(tile, halo, axis, -2)
-            return near * (after - tile) + far * (after_two - before)
+            return near * (after - tile) + (after_two - before)
         before_two = shifted(tile, halo, axis, 2)
-        return near * (tile - before) + far * (after - before_two)
+        return near * (tile - before) + (after - before_two)
 
     def differ_z(ref, field, z, forward):
         at = [ref[field, z + 2 + k] for k in ((-1, 0, 1, 2) if forward else (-2, -1, 0, 1))]
-        return near * (at[2] - at[1]) + far * (at[3] - at[0])
+        return near * (at[2] - at[1]) + (at[3] - at[0])
 
     def weight(mask, value):
         return jnp.where(mask, jnp.float32(value), jnp.float32(0.0))
@@ -351,14 +350,14 @@
         before, after = turned(tile, 1, axis), turned(tile, -1, axis)
         if forward:
             return (
-                weight(low_one, -far) * before
+                weight(low_one, -1.0) * before
                 + weight(high_one, near) * after
-                + weight(high_two, far) * turned(tile, -2, axis)
+                + weight(high_two, 1.0) * turned(tile, -2, axis)
             )
         return (
             weight(low_one, -near) * before
-            + weight(low_two, -far) * turned(tile, 2, axis)
-            + weight(high_one, far) * after
+            + weight(low_two, -1.0) * turned(tile, 2, axis)
+            + weight(high_one, 1.0) * after
         )
 
     row_ends = (row_at < 1, row_at < 2, row_at >= 7, row_at >= 6)
@@ -369,19 +368,19 @@
         low_one, low_two, high_one, high_two = row_ends
         if forward:
             two = turned(tile, -2, 0)
-            whole = near * (after - tile) + far * (two - before)
+            whole = near * (after - tile) + (two - before)
             wrap = (
-                weight(low_one, -far) * before
+                weight(low_one, -1.0) * before
                 + weight(high_one, near) * after
-                + weight(high_two, far) * two
+                + weight(high_two, 1.0) * two
             )
         else:
             two = turned(tile, 2, 0)
-            whole = near * (tile - before) + far * (after - two)
+            whole = near * (tile - before) + (after - two)
             wrap = (
                 weight(low_one, -near) * before
-                + weight(low_two, -far) * two
-                + weight(high_one, far) * after
+                + weight(low_two, -1.0) * two
+                + weight(high_one, 1.0) * after
             )
         return whole - wrap, wrap
 
@@ -392,15 +391,15 @@
             return (
                 weight(lane_at < 127, near) * after
                 - near * tile
-                + weight(lane_at < 126, far) * two
-                - weight(lane_at >= 1, far) * before
+                + jnp.where(lane_at < 126, two, 0.0)
+                - jnp.where(lane_at >= 1, before, 0.0)
             )
         two = turned(tile, 2, 1)
         return (
             near * tile
             - weight(lane_at >= 1, near) * before
-            + weight(lane_at < 127, far) * after
-            - weight(lane_at >= 2, far) * two
+            + jnp.where(lane_at < 127, after, 0.0)
+            - jnp.where(lane_at >= 2, two, 0.0)
         )
 
     def push_chunk(step, pair, sub, stress, speed):

time: 24.9 us -> 24.8 us (level)
  no operation moved by 1% of the time
where the time goes in v6:
time: 24.8 us; the launch traced here: 24.7 us
  Pallas kernels  24.1 us (97%)
  between operations  0.64 us (3%)
    pallas_call x1, Pallas kernels, local(): pl.pallas_call(functools.partial(kernel, counts), out_shape=(pltpu.VMEM(f...  23.1 us
    pallas_call x1, Pallas kernels, local(): pl.pallas_call(hand_on, out_shape=(jax.ShapeDtypeStruct(fields.shape, f32...  1.03 us

profile of v6, /device:TPU:27, one launch (start us, length us, event | category | flops | bytes accessed | tf_op | source)
XLA Modules:
  0.0 24.7 jit_solution(753294013955047250)
XLA Ops:
  0.6 23.1 %waves.1 = (f32[9,32,8,128]{3,2,1,0:T(8,128)S(1)}, f32[3,8,128]{2,1,0:T(8,128)S(1)}) custom-call(f32[9,32,8,128]{3,2,1,0:T(8,128)} %fields_ref.1, f32[32,8,128]{2,1,0:T(8,128)} %lame_ref.1, f32[32,8,128]{2,1,0:T(8,128)} %shear_ref.1, f32[32,8,128]{2,1,0:T(8,128)} %buoy_ref.1, f32[3,8,128]{2,1,0:T(8,128)} %ocean_ref.1, f32[8,128]{1,0:T(8,128)} %depth_ref.1, ...), custom_call_target="tpu_custom_call" | custom-call | tf_op jit(solution)/shard_map/waves/pallas_call | solution.py:723
  23.7 1.0 %hand_on.1 = (f32[9,32,8,128]{3,2,1,0:T(8,128)}, f32[3,8,128]{2,1,0:T(8,128)}) custom-call(f32[9,32,8,128]{3,2,1,0:T(8,128)S(1)} %get-tuple-element.4.waves, f32[3,8,128]{2,1,0:T(8,128)S(1)} %get-tuple-element.5.sea), custom_call_target="tpu_custom_call" | custom-call | tf_op jit(solution)/shard_map/hand_on/pallas_call | solution.py:776
